TPU v7x, 32 devices: a whole 2x2x4 slice. The times are simulated.
32 devices in a mesh: grp: 2 (over y), gx: 4 (over z), gy: 2 (over x), gz: 2 (over core).
Axes of the slice: x: 2, y: 2, z: 4, core: 2. Of those that a mesh axis runs over, the one named last changes fastest.
Arguments:
- controls: float32 [40, 64, 512], P('gz', ('grp', 'gx'), 'gy'), parts along dimension 1, may hold values from -8.1 to 8.1
- anomalies: bfloat16 [2, 40, 64, 512], P(None, 'gz', ('grp', 'gx'), 'gy'), parts along dimension 2, may hold values from -6 to 6
- x_rates: float32 [64, 512], P(('grp', 'gx'), 'gy'), parts along dimension 0, may hold values from 0.3 to 1
- y_rates: float32 [64, 512], P(('grp', 'gx'), 'gy'), parts along dimension 0, may hold values from 0.3 to 1
- obs_cells: int32 [8, 2, 512], P(('grp', 'gx'), 'gy'), parts along dimension 0, may hold values from 0 to 2047
- obs_codes: int32 [8, 2, 512], P(('grp', 'gx'), 'gy'), parts along dimension 0, may hold values from 0 to 71
- obs_values: float32 [8, 2, 512], P(('grp', 'gx'), 'gy'), parts along dimension 0, may hold values from -6 to 6
- obs_weights: float32 [8, 2, 512], P(('grp', 'gx'), 'gy'), parts along dimension 0, may hold values from 0.25 to 4
- prev_gradient: float32 [40, 64, 512], P('gz', ('grp', 'gx'), 'gy'), parts along dimension 1, may hold values from -8.1 to 8.1
- prev_direction: float32 [40, 64, 512], P('gz', ('grp', 'gx'), 'gy'), parts along dimension 1, may hold values from -6 to 6
Outputs:
- gradient: float32 [40, 64, 512], P('gz', ('grp', 'gx'), 'gy'), parts along dimension 1
- direction: float32 [40, 64, 512], P('gz', ('grp', 'gx'), 'gy'), parts along dimension 1
- increment: float32 [2, 64, 512], P(None, ('grp', 'gx'), 'gy'), parts along dimension 1
There are 2 independent parts, one for each index of `grp`. A program takes and returns all parts, laid end to end along the dimension named above; each array names one. Nothing has to cross between parts.
Inputs may be any that keep to these rules, and one draw needn't show every extreme that they name: obs_cells holds x * 256 + y for the cell (x, y) of the tile.
All inputs are finite; a program needn't handle non-finite values.
Results may differ from a plain program's by a relative error of at most 0.0003.
Values sent between devices are 32-bit elements; how exact they have to be, the bound alone decides.
No kernel may reach another device: no remote copies, remote signals or barrier semaphores. Data moves between devices by JAX's collectives and lax.ppermute only.
A program may use at most 128 MiB of HBM per device.

v0:
```python
import math

import jax
import jax.numpy as jnp
from jax import lax
from jax.sharding import PartitionSpec as P

K = 40
NDIR = 72


def prefix(part, axis, combine, identity, reverse):
    count = lax.axis_size(axis)
    place = lax.axis_index(axis)
    ahead = count - 1 - place if reverse else place
    gathered = jax.tree.map(lambda a: lax.all_gather(a, axis), part)
    state = jax.tree.map(lambda a, e: jnp.zeros_like(a) + jnp.asarray(e, a.dtype), part, identity)

    def one(turn, state):
        source = count - 1 - turn if reverse else turn
        return combine(
            state, jax.tree.map(lambda a: lax.dynamic_index_in_dim(a, source, 0, False), gathered)
        )

    return lax.fori_loop(0, ahead, one, state)


def compose(earlier, latter):
    first_mult, first_add = earlier
    second_mult, second_add = latter
    return (first_mult * second_mult, second_mult * first_add + second_add)


def local_run(factor_field, weights, along_dim, reverse):
    spread_field = jnp.broadcast_to(factor_field, weights.shape)
    return lax.associative_scan(compose, (spread_field, weights), reverse=reverse, axis=along_dim)


def chain_states(factor_field, weights, along_dim, reverse):
    products, states = local_run(factor_field, weights, along_dim, reverse)
    boundary = 0 if reverse else weights.shape[along_dim] - 1
    total_mult = lax.index_in_dim(products[0:1], boundary, along_dim, keepdims=False)
    total_add = lax.index_in_dim(states, boundary, along_dim, keepdims=False)
    neutral = (jnp.ones_like(total_mult), jnp.zeros_like(total_add))
    if along_dim == 1:
        _, incoming = prefix((total_mult, total_add), "gx", compose, neutral, reverse)
    else:
        _, incoming = prefix((total_mult, total_add), "gy", compose, neutral, reverse)
    return states + products * jnp.expand_dims(incoming, along_dim)


def smooth(factor_field, gain_field, values, along_dim, adjoint, runner):
    leading = factor_field * values if adjoint else gain_field * values
    inward = runner(factor_field, leading, along_dim, False)
    outward = runner(factor_field, gain_field * inward, along_dim, True)
    return gain_field / factor_field * outward if adjoint else outward


def shards(
    controls,
    anomalies,
    x_rates,
    y_rates,
    obs_cells,
    obs_codes,
    obs_values,
    obs_weights,
    prev_gradient,
    prev_direction,
):
    x_factor = x_rates[None]
    y_factor = y_rates[None]
    x_scales = jnp.sqrt(1.0 - x_factor * x_factor)
    y_scales = jnp.sqrt(1.0 - y_factor * y_factor)
    spread = 1.0 / math.sqrt(K - 1)

    def pass_first(values, adjoint):
        return smooth(x_factor, x_scales, values, 1, adjoint, chain_states)

    def pass_second(values, adjoint):
        return smooth(y_factor, y_scales, values, 2, adjoint, chain_states)

    filtered = pass_second(pass_first(controls, False), False)
    partial_value = jnp.sum(anomalies.astype(jnp.float32) * filtered[None], axis=1) * spread
    increment = lax.psum(partial_value, "gz")
    located = obs_cells.reshape(-1)
    bearing = obs_codes.reshape(-1).astype(jnp.float32) * (2.0 * math.pi / NDIR)
    cosine = jnp.cos(bearing)
    sines = jnp.sin(bearing)
    flat_east = increment[0].reshape(-1)
    flat_north = increment[1].reshape(-1)
    projected = cosine * flat_east[located] + sines * flat_north[located]
    misfit = obs_weights.reshape(-1) * (projected - obs_values.reshape(-1))
    cell_count = flat_east.shape[0]
    back_east = (
        jnp.zeros((cell_count,), jnp.float32)
        .at[located]
        .add(cosine * misfit)
        .reshape(increment.shape[1:])
    )
    back_north = (
        jnp.zeros((cell_count,), jnp.float32)
        .at[located]
        .add(sines * misfit)
        .reshape(increment.shape[1:])
    )
    pulled = (
        anomalies[0].astype(jnp.float32) * back_east[None]
        + anomalies[1].astype(jnp.float32) * back_north[None]
    ) * spread
    gradient = controls + pass_first(pass_second(pulled, True), True)
    numerator, denominator = lax.psum(
        (jnp.sum(gradient * (gradient - prev_gradient)), jnp.sum(prev_gradient * prev_gradient)),
        ("gx", "gy", "gz"),
    )
    direction = -gradient + numerator / denominator * prev_direction
    return (gradient, direction, increment)


def solution(mesh):
    in_specs = (
        P("gz", ("grp", "gx"), "gy"),
        P(None, "gz", ("grp", "gx"), "gy"),
        P(("grp", "gx"), "gy"),
        P(("grp", "gx"), "gy"),
        P(("grp", "gx"), "gy", None),
        P(("grp", "gx"), "gy", None),
        P(("grp", "gx"), "gy", None),
        P(("grp", "gx"), "gy", None),
        P("gz", ("grp", "gx"), "gy"),
        P("gz", ("grp", "gx"), "gy"),
    )
    out_specs = (
        P("gz", ("grp", "gx"), "gy"),
        P("gz", ("grp", "gx"), "gy"),
        P(None, ("grp", "gx"), "gy"),
    )
    return jax.shard_map(shards, mesh=mesh, in_specs=in_specs, out_specs=out_specs, check_vma=False)
```

profile of v0, /device:TPU:0, one launch (start us, length us, event | category | flops | bytes accessed | tf_op | source)
XLA Modules:
  0.0 457.4 jit_solution(16847866725613544336)
XLA Ops:
  5.6 14.9 %all-gather = f32[80,1,256]{2,1,0:T(1,128)S(1)} all-gather(f32[20,1,256]{2,1,0:T(1,128)S(1)} %slice_add_fusion.21), channel_id=2, replica_groups=mesh['grp'=2,'gx'=4,'gy'=2,'gz'=2] {'gx'}, dimensions={0}, use_global_device_ids=true | all-gather | bytes 102400 | tf_op jit(solution)/shard_map/all_gather | solution.py:16
  21.2 11.1 %all_gather.40 = f32[4,1,256]{2,1,0:T(1,128)S(1)} all-gather(f32[1,1,256]{2,1,0:T(1,128)S(1)} %slice_add_fusion.27), channel_id=1, replica_groups=mesh['grp'=2,'gx'=4,'gy'=2,'gz'=2] {'gx'}, dimensions={0}, use_global_device_ids=true | all-gather | bytes 5120 | tf_op jit(solution)/shard_map/all_gather | solution.py:16
  36.5 13.2 %all-gather.1 = f32[80,1,256]{2,1,0:T(1,128)S(1)} all-gather(f32[20,1,256]{2,1,0:T(1,128)S(1)} %slice_add_fusion.18), channel_id=3, replica_groups=mesh['grp'=2,'gx'=4,'gy'=2,'gz'=2] {'gx'}, dimensions={0}, use_global_device_ids=true | all-gather | bytes 102400 | tf_op jit(solution)/shard_map/all_gather | solution.py:16
  50.4 7.6 %all_gather.42 = f32[4,1,256]{2,1,0:T(1,128)S(1)} all-gather(f32[1,1,256]{2,1,0:T(1,128)S(1)} %slice_add_fusion.26), channel_id=1, replica_groups=mesh['grp'=2,'gx'=4,'gy'=2,'gz'=2] {'gx'}, dimensions={0}, use_global_device_ids=true | all-gather | bytes 5120 | tf_op jit(solution)/shard_map/all_gather | solution.py:16
  59.4 2.7 slice.1306
  62.2 2.8 slice.1307
  99.1 14.4 %pad.503 = f32[20,8,32]{2,1,0:T(8,128)S(1)} pad(f32[20,8,16]{2,1,0:T(8,128)S(1)} %add.982, f32[]{:T(128)} %constant.182.clone.1), padding=0_0_0x0_0_0x1_0_1 | pad | bytes 30724 | tf_op jit(solution)/shard_map/pad | solution.py:36
  114.5 2.0 pad.488
  116.5 2.0 pad.489
  118.6 2.0 pad.505
  120.9 2.0 pad.504
  124.6 2.7 pad.490
  127.4 2.7 pad.491
  130.1 4.0 pad.493
  134.4 2.7 pad.506
  137.2 2.7 pad.507
  139.9 2.7 slice.1363
  143.0 4.0 pad.492
  147.3 4.4 all-gather.3
  151.9 4.0 pad.509
  156.3 4.0 pad.508
  160.5 4.2 all-gather.2
  164.9 2.7 slice.1393
  167.8 2.8 slice.1395
  212.6 2.0 pad.520
  214.6 2.0 pad.521
  216.7 2.0 pad.537
  223.8 2.7 pad.522
  226.5 2.7 pad.523
  229.3 4.0 pad.525
  233.4 2.7 pad.538
  236.1 2.7 pad.539
  238.9 2.7 slice.1450
  242.2 4.0 pad.524
  246.6 4.4 all-gather.5
  251.1 4.0 pad.541
  255.4 4.0 pad.540
  259.6 4.2 all-gather.4
  265.6 3.4 psum.21
  269.6 3.1 gather_fusion
  272.8 3.1 gather_fusion.1
  276.8 3.3 scatter_custom_fusion
  280.1 3.3 scatter_custom_fusion.1
  283.4 2.7 slice.1474
  286.2 2.7 slice.1475
  309.2 2.0 pad.553
  315.6 2.7 pad.554
  318.4 2.7 pad.555
  321.1 4.0 pad.557
  325.2 2.7 slice.1509
  328.0 4.0 pad.556
  332.4 4.4 all-gather.6
  337.5 2.7 slice.1512
  340.3 2.8 slice.1514
  363.4 2.0 pad.569
  369.9 2.7 pad.570
  372.6 2.7 pad.571
  375.4 4.0 pad.573
  379.4 2.7 slice.1549
  382.5 4.0 pad.572
  386.8 4.4 all-gather.7
  393.8 13.2 %all-gather.8 = f32[80,1,256]{2,1,0:T(1,128)S(1)} all-gather(f32[20,1,256]{2,1,0:T(1,128)S(1)} %slice_add_fusion.15), channel_id=10, replica_groups=mesh['grp'=2,'gx'=4,'gy'=2,'gz'=2] {'gx'}, dimensions={0}, use_global_device_ids=true | all-gather | bytes 102400 | tf_op jit(solution)/shard_map/all_gather | solution.py:16
  409.8 13.2 %all-gather.9 = f32[80,1,256]{2,1,0:T(1,128)S(1)} all-gather(f32[20,1,256]{2,1,0:T(1,128)S(1)} %slice_add_fusion.12), channel_id=11, replica_groups=mesh['grp'=2,'gx'=4,'gy'=2,'gz'=2] {'gx'}, dimensions={0}, use_global_device_ids=true | all-gather | bytes 102400 | tf_op jit(solution)/shard_map/all_gather | solution.py:16
  425.2 30.1 %all-reduce.132 = (f32[]{:T(128)}, f32[]{:T(128)}) all-reduce(f32[]{:T(128)} %get-tuple-element.604, f32[]{:T(128)} %get-tuple-element.603), channel_id=1, replica_groups=mesh['grp'=2,'gx'=4,'gy'=2,'gz'=2] {'gx','gy','gz'}, use_global_device_ids=true, to_apply=%region_21.22 | all-reduce | flops 2 | bytes 16 | tf_op jit(solution)/shard_map/psum | solution.py:112
  (599 shorter events, 160.2 us)
Async XLA Ops:
  2.4 0.7 copy-start.5
  58.7 0.7 copy-start.6
  264.7 0.9 copy-start
  264.7 4.9 %copy-start.9 = (s32[1,1,512]{2,1,0:T(1,128)S(1)}, s32[1,1,512]{2,1,0:T(1,128)}, u32[]{:S(2)}) copy-start(s32[1,1,512]{2,1,0:T(1,128)} %param.30) | copy-start | bytes 6148
  269.0 0.6 copy-start.7
  272.8 3.2 copy-start.8
  276.0 0.7 copy-start.11
  276.1 0.7 copy-start.10
  423.4 0.9 copy-start.1
  423.5 1.0 copy-start.4
  424.4 32.1 %copy-start.3 = (f32[20,8,256]{2,1,0:T(8,128)S(1)}, f32[20,8,256]{2,1,0:T(8,128)}, u32[]{:S(2)}) copy-start(f32[20,8,256]{2,1,0:T(8,128)} %param.35) | copy-start | bytes 491524
  425.2 32.1 %copy-start.2 = (f32[20,8,256]{2,1,0:T(8,128)}, f32[20,8,256]{2,1,0:T(8,128)S(1)}, u32[]{:S(2)}) copy-start(f32[20,8,256]{2,1,0:T(8,128)S(1)} %get-tuple-element.694) | copy-start | bytes 491524
where the time goes:
time: 455 us; the launch traced here: 457 us
  local copies, waits for them, and re-layouts  297 us (65%)
  blocking collectives  133 us (29%)
  other arithmetic  21.3 us (5%)
  between operations  5.37 us (1%)
    pad x108, local copies, waits for them, and re-layouts, local_run(): lax.associative_scan(compose, (spread_field, weights), reverse=reverse, a...  196 us
    all_gather x12, blocking collectives, prefix(): gathered = jax.tree.map(lambda a: lax.all_gather(a, axis), part)  99.2 us
    slice x181, local copies, waits for them, and re-layouts, local_run(): lax.associative_scan(compose, (spread_field, weights), reverse=reverse, a...  86.7 us
    psum x1, blocking collectives, shards(): lax.psum((jnp.sum(gradient * (gradient - prev_gradient)), jnp.sum(prev_gr...  30.1 us

commit v1 on v0

v1 whole, which is shorter than its diff:
```python
import functools
import math

import jax
import jax.numpy as jnp
from jax import lax
from jax.experimental import pallas as pl
from jax.experimental.pallas import tpu as pltpu
from jax.sharding import PartitionSpec as P

NDIR = 72
SUB = 8
LANES = 128
VMEM_SPEC = pl.BlockSpec(memory_space=pltpu.VMEM)


def call(body, out_shape, scratch=(), flops=100000, moved=100000):
    return pl.pallas_call(
        body,
        out_shape=out_shape,
        scratch_shapes=list(scratch),
        cost_estimate=pl.CostEstimate(flops=flops, bytes_accessed=moved, transcendentals=0),
    )


def f32(*shape):
    return jax.ShapeDtypeStruct(shape, jnp.float32)


def row_count(members):
    return -(-(members + 1) // SUB) * SUB


def chain(get, count, place):
    first = get(0)
    entering = jnp.zeros_like(first[0])
    if count == 1:
        return entering, entering
    for d in range(count - 1, 0, -1):
        out, _, product, _ = get(d)
        entering = jnp.where(place >= d, out + product * entering, entering)
    at = {}
    state = first[0] + first[2] * entering
    for d in range(1, count):
        at[d] = state
        if d < count - 1:
            out, _, product, _ = get(count - d)
            state = out + product * state
    backward = jnp.zeros_like(entering)
    for d in range(count - 1, 0, -1):
        _, out, product, response = get(count - d)
        backward = jnp.where(place + d < count, out + response * at[d] + product * backward, backward)
    return entering, backward


def source_reader(refs, count, axis):
    if len(refs) == count:
        return lambda d: refs[d][...]
    place = lax.axis_index(axis)
    return lambda d: refs[0][lax.rem(place - d + count, count)]


def x_reader(refs, count, axis, members):
    read = source_reader(refs, count, axis)
    half = row_count(members)

    def get(d):
        block = read(d)
        out, back = block[:half], block[half:]
        return out, back, out[members : members + 1], back[members : members + 1]

    return get


def y_reader(refs, count, axis, members):
    read = source_reader(refs, count, axis)
    half = LANES // 2

    def get(d):
        block = read(d)
        back = pltpu.roll(block, half, 1)
        return (
            block,
            back,
            jnp.broadcast_to(block[:, members : members + 1], block.shape),
            jnp.broadcast_to(back[:, members : members + 1], block.shape),
        )

    return get


def tables_of(rates, axis, reverse):
    width = rates.shape[axis]
    at = lax.broadcasted_iota(jnp.int32, rates.shape, axis)
    table = jnp.where(at == (width - 1 if reverse else 0), 0.0, rates)
    tables, step = [], 1
    while step < width:
        tables.append(table)
        table = table * pltpu.roll(table, width - step if reverse else step, axis)
        step *= 2
    return tables


def sweep(values, tables, axis, reverse):
    width = values.shape[axis]
    step = 1
    for table in tables:
        values = values + table * pltpu.roll(values, width - step if reverse else step, axis)
        step *= 2
    return values


def responses(rates, scales, axis, forward, reverse):
    at = lax.broadcasted_iota(jnp.int32, rates.shape, axis)
    product = sweep(jnp.where(at == 0, rates, 0.0), forward, axis, False)
    answer = sweep(scales * product, reverse, axis, True)
    behind = sweep(jnp.where(at == rates.shape[axis] - 1, rates, 0.0), reverse, axis, True)
    return product, answer, behind


def x_sweeps(get, count, rates, scales, store, message_ref):
    rows = rates.shape[0]
    half = row_count(count)
    forward, reverse = tables_of(rates, 0, False), tables_of(rates, 0, True)
    product, answer, behind = responses(rates, scales, 0, forward, reverse)
    store(count, answer)
    store(count + 1, behind)
    message_ref[count:half] = jnp.zeros((half - count, rates.shape[1]), jnp.float32)
    message_ref[half + count :] = jnp.zeros((half - count, rates.shape[1]), jnp.float32)
    message_ref[count : count + 1] = product[rows - 1 :]
    message_ref[half + count : half + count + 1] = answer[:1]
    for k in range(count):
        ahead = sweep(get(k), forward, 0, False)
        back = sweep(scales * ahead, reverse, 0, True)
        store(k, back)
        message_ref[k : k + 1] = ahead[rows - 1 :]
        message_ref[half + k : half + k + 1] = back[:1]


def y_sweeps(get, count, scales, forward, reverse, store, message_ref, products):
    rows, columns = scales.shape
    lane = lax.broadcasted_iota(jnp.int32, (rows, LANES), 1)
    half = LANES // 2
    message = jnp.where(lane == count, products[0], jnp.where(lane == half + count, products[1], 0.0))
    for k in range(count):
        ahead = sweep(get(k), forward, 1, False)
        back = sweep(scales * ahead, reverse, 1, True)
        store(k, back)
        message = jnp.where(lane == k, ahead[:, columns - 1 :], message)
        message = jnp.where(lane == half + k, back[:, :1], message)
    message_ref[...] = message


def split_dot(a, b, dims):
    rows = a.shape[0]
    high = a.astype(jnp.bfloat16)
    rest = a - high.astype(jnp.float32)
    middle = rest.astype(jnp.bfloat16)
    low = (rest - middle.astype(jnp.float32)).astype(jnp.bfloat16)
    parts = jnp.concatenate([high, middle, low], axis=0)
    out = lax.dot_general(parts, b, (dims, ((), ())), preferred_element_type=jnp.float32)
    return out[:rows] + (out[rows : 2 * rows] + out[2 * rows :])


def storer(ref):
    def store(k, value):
        ref[k] = value

    return store


def table_refs(ref):
    return [ref[n] for n in range(ref.shape[0])]


def first_kernel(members, controls_ref, rates_ref, local_ref, message_ref):
    rates = rates_ref[...]
    scales = jnp.sqrt(1.0 - rates * rates)
    x_sweeps(lambda k: scales * controls_ref[k], members, rates, scales, storer(local_ref), message_ref)


def tables_kernel(
    rates_ref, cells_ref, codes_ref, old_ref, forward_ref, reverse_ref, response_ref, columns_ref, weights_ref, old_sum_ref
):
    rates = rates_ref[...]
    rows, columns = rates.shape
    scales = jnp.sqrt(1.0 - rates * rates)
    forward, reverse = tables_of(rates, 1, False), tables_of(rates, 1, True)
    for n in range(len(forward)):
        forward_ref[n] = forward[n]
        reverse_ref[n] = reverse[n]
    for n, value in enumerate(responses(rates, scales, 1, forward, reverse)):
        response_ref[n] = value
    cells = cells_ref[...]
    count = cells.shape[1]
    at = lax.broadcasted_iota(jnp.int32, (columns, count), 0)
    columns_ref[...] = jnp.where(at == cells % columns, 1.0, 0.0).astype(jnp.bfloat16)
    bearing = codes_ref[...].astype(jnp.float32) * (2.0 * math.pi / NDIR)
    row = lax.broadcasted_iota(jnp.int32, (rows, count), 0) == cells // columns
    weights_ref[:rows] = jnp.where(row, jnp.cos(bearing), 0.0)
    weights_ref[rows:] = jnp.where(row, jnp.sin(bearing), 0.0)
    total = jnp.zeros((rows, columns), jnp.float32)
    for k in range(old_ref.shape[0]):
        total += old_ref[k] * old_ref[k]
    old_sum_ref[...] = total


def second_kernel(members, count, *refs):
    messages = refs[: -8]
    local_ref, rates_ref, forward_ref, reverse_ref, response_ref, out_ref, message_ref, states_ref = refs[-8:]
    rows, columns = rates_ref.shape
    place = lax.axis_index("gx")
    entering, backward = chain(x_reader(messages, count, "gx", members), count, place)
    half = row_count(members)
    states_ref[:half] = entering
    states_ref[half:] = backward
    y_rates = rates_ref[...]
    scales = jnp.sqrt(1.0 - y_rates * y_rates)
    ahead, behind = local_ref[members], local_ref[members + 1]

    def get(k):
        return scales * (local_ref[k] + ahead * states_ref[k : k + 1] + behind * states_ref[half + k : half + k + 1])

    products = (response_ref[0][:, columns - 1 :], response_ref[1][:, :1])
    forward, reverse = table_refs(forward_ref), table_refs(reverse_ref)
    y_sweeps(get, members, scales, forward, reverse, storer(out_ref), message_ref, products)


def third_kernel(members, count, spread, *refs):
    messages = refs[:-4]
    local_ref, response_ref, anomalies_ref, out_ref = refs[-4:]
    entering, backward = chain(y_reader(messages, count, "gy", members), count, lax.axis_index("gy"))
    ahead, behind = response_ref[1], response_ref[2]
    rows = ahead.shape[0]
    east, north = jnp.zeros_like(ahead), jnp.zeros_like(ahead)
    for k in range(members):
        filtered = local_ref[k] + ahead * entering[:, k : k + 1] + behind * backward[:, k : k + 1]
        east += anomalies_ref[0, k].astype(jnp.float32) * filtered
        north += anomalies_ref[1, k].astype(jnp.float32) * filtered
    out_ref[:rows] = east * spread
    out_ref[rows:] = north * spread


def fourth_kernel(members, spread, shares, *refs):
    partials = refs[:shares]
    (
        anomalies_ref,
        columns_ref,
        weights_ref,
        values_ref,
        precisions_ref,
        rates_ref,
        forward_ref,
        reverse_ref,
        response_ref,
        increment_ref,
        out_ref,
        message_ref,
    ) = refs[shares:]
    rates = rates_ref[...]
    rows, columns = rates.shape
    increment = partials[0][...]
    for ref in partials[1:]:
        increment = increment + ref[...]
    increment_ref[...] = increment
    picked = split_dot(increment, columns_ref[...], ((1,), (0,)))
    weights = weights_ref[...]
    projected = jnp.sum(weights * picked, axis=0, keepdims=True)
    misfit = precisions_ref[...] * (projected - values_ref[...])
    back = split_dot(weights * misfit, columns_ref[...], ((1,), (1,)))
    scales = jnp.sqrt(1.0 - rates * rates)
    east = back[:rows] * rates * spread
    north = back[rows:] * rates * spread

    def get(k):
        return anomalies_ref[0, k].astype(jnp.float32) * east + anomalies_ref[1, k].astype(jnp.float32) * north

    products = (response_ref[0][:, columns - 1 :], response_ref[1][:, :1])
    forward, reverse = table_refs(forward_ref), table_refs(reverse_ref)
    y_sweeps(get, members, scales, forward, reverse, storer(out_ref), message_ref, products)


def fifth_kernel(members, count, *refs):
    messages = refs[:-6]
    local_ref, response_ref, y_rates_ref, x_rates_ref, out_ref, message_ref = refs[-6:]
    entering, backward = chain(y_reader(messages, count, "gy", members), count, lax.axis_index("gy"))
    y_rates, x_rates = y_rates_ref[...], x_rates_ref[...]
    factor = x_rates * jnp.sqrt(1.0 - y_rates * y_rates) / y_rates
    ahead, behind = factor * response_ref[1], factor * response_ref[2]

    def get(k):
        return factor * local_ref[k] + ahead * entering[:, k : k + 1] + behind * backward[:, k : k + 1]

    x_sweeps(get, members, x_rates, jnp.sqrt(1.0 - x_rates * x_rates), storer(out_ref), message_ref)


def sixth_kernel(members, count, *refs):
    messages = refs[:-8]
    local_ref, rates_ref, controls_ref, old_ref, old_sum_ref, gradient_ref, sums_ref, states_ref = refs[-8:]
    entering, backward = chain(x_reader(messages, count, "gx", members), count, lax.axis_index("gx"))
    half = row_count(members)
    states_ref[:half] = entering
    states_ref[half:] = backward
    rates = rates_ref[...]
    rows, columns = rates.shape
    factor = jnp.sqrt(1.0 - rates * rates) / rates
    ahead, behind = factor * local_ref[members], factor * local_ref[members + 1]
    total = jnp.zeros((rows, columns), jnp.float32)
    for k in range(members):
        gradient = controls_ref[k] + (
            factor * local_ref[k] + ahead * states_ref[k : k + 1] + behind * states_ref[half + k : half + k + 1]
        )
        gradient_ref[k] = gradient
        total += gradient * (gradient - old_ref[k])
    sums_ref[:rows] = total
    sums_ref[rows:] = old_sum_ref[...]


def last_kernel(stacked, *refs):
    sums = refs[:-3]
    gradient_ref, old_ref, direction_ref = refs[-3:]
    if stacked:
        total = jnp.sum(sums[0][...], axis=0)
    else:
        total = sums[0][...]
        for ref in sums[1:]:
            total = total + ref[...]
    half = total.shape[0] // 2
    numerator = jnp.sum(total[:half], axis=(0, 1), keepdims=True)
    denominator = jnp.sum(total[half:], axis=(0, 1), keepdims=True)
    ratio = numerator / denominator
    for k in range(gradient_ref.shape[0]):
        direction_ref[k] = ratio * old_ref[k] - gradient_ref[k]


def exchange(message, axis, count):
    if count <= 4:
        shifts = range(1, count)
        return [message] + [lax.ppermute(message, axis, [(i, (i + d) % count) for i in range(count)]) for d in shifts]
    return [lax.all_gather(message, axis)]


def add_over(values, axis, count):
    if count == 2:
        return values + lax.ppermute(values, axis, [(0, 1), (1, 0)])
    return lax.psum(values, axis)


def shards(
    n_gx,
    n_gy,
    n_gz,
    controls,
    anomalies,
    x_rates,
    y_rates,
    obs_cells,
    obs_codes,
    obs_values,
    obs_weights,
    prev_gradient,
    prev_direction,
):
    members, rows, columns = controls.shape
    spread = 1.0 / math.sqrt(members * n_gz - 1)
    lines = 2 * row_count(members)
    observed = obs_cells.size
    depth = (columns - 1).bit_length()
    field = (members, rows, columns)
    extended = (members + 2, rows, columns)

    local, message = call(
        functools.partial(first_kernel, members), (f32(*extended), f32(lines, columns))
    )(controls, x_rates)
    x_messages = exchange(message, "gx", n_gx)
    forward, reverse, response, column_ones, row_weights, old_sum = call(
        tables_kernel,
        (
            f32(depth, rows, columns),
            f32(depth, rows, columns),
            f32(3, rows, columns),
            jax.ShapeDtypeStruct((columns, observed), jnp.bfloat16),
            f32(2 * rows, observed),
            f32(rows, columns),
        ),
    )(y_rates, obs_cells.reshape(1, observed), obs_codes.reshape(1, observed), prev_gradient)
    filtered, message = call(
        functools.partial(second_kernel, members, n_gx),
        (f32(*field), f32(rows, LANES)),
        [pltpu.VMEM((lines, columns), jnp.float32)],
    )(*x_messages, local, y_rates, forward, reverse, response)
    partial = call(functools.partial(third_kernel, members, n_gy, spread), f32(2 * rows, columns))(
        *exchange(message, "gy", n_gy), filtered, response, anomalies
    )
    if n_gz == 2:
        partials = [partial, lax.ppermute(partial, "gz", [(0, 1), (1, 0)])]
    else:
        partials = [lax.psum(partial, "gz")]
    increment, pulled, message = call(
        functools.partial(fourth_kernel, members, spread, len(partials)),
        (f32(2 * rows, columns), f32(*field), f32(rows, LANES)),
    )(
        *partials,
        anomalies,
        column_ones,
        row_weights,
        obs_values.reshape(1, observed),
        obs_weights.reshape(1, observed),
        y_rates,
        forward,
        reverse,
        response,
    )
    local, message = call(
        functools.partial(fifth_kernel, members, n_gy),
        (f32(*extended), f32(lines, columns)),
    )(*exchange(message, "gy", n_gy), pulled, response, y_rates, x_rates)
    gradient, sums = call(
        functools.partial(sixth_kernel, members, n_gx),
        (f32(*field), f32(2 * rows, columns)),
        [pltpu.VMEM((lines, columns), jnp.float32)],
    )(*exchange(message, "gx", n_gx), local, x_rates, controls, prev_gradient, old_sum)
    sums = add_over(add_over(sums, "gz", n_gz), "gy", n_gy)
    totals = exchange(sums, "gx", n_gx)
    direction = call(functools.partial(last_kernel, len(totals) != n_gx), f32(*field))(
        *totals, gradient, prev_direction
    )
    return gradient, direction, increment.reshape(2, rows, columns)


def solution(mesh):
    in_specs = (
        P("gz", ("grp", "gx"), "gy"),
        P(None, "gz", ("grp", "gx"), "gy"),
        P(("grp", "gx"), "gy"),
        P(("grp", "gx"), "gy"),
        P(("grp", "gx"), "gy", None),
        P(("grp", "gx"), "gy", None),
        P(("grp", "gx"), "gy", None),
        P(("grp", "gx"), "gy", None),
        P("gz", ("grp", "gx"), "gy"),
        P("gz", ("grp", "gx"), "gy"),
    )
    out_specs = (
        P("gz", ("grp", "gx"), "gy"),
        P("gz", ("grp", "gx"), "gy"),
        P(None, ("grp", "gx"), "gy"),
    )
    body = functools.partial(shards, mesh.shape["gx"], mesh.shape["gy"], mesh.shape["gz"])
    return jax.shard_map(body, mesh=mesh, in_specs=in_specs, out_specs=out_specs, check_vma=False)
```

time: 455 us -> 60.8 us (0.13)
  local copies, waits for them, and re-layouts: 297 us -> 3.63 us
  blocking collectives: 133 us -> 0 us
  waiting for transfers between devices: 0 us -> 20.7 us
  other arithmetic: 21.3 us -> 0.73 us
  Pallas kernels: 0 us -> 18.2 us
  starting transfers between devices: 0 us -> 16.5 us
  between operations: 5.37 us -> 0.68 us
    pad x108 -> x0, local copies, waits for them, and re-layouts: 196 us -> none  [local_run(): lax.associative_scan(compose, (spread_field, weights), reverse=reverse, a...]
    all_gather x12 -> x0, blocking collectives: 99.2 us -> none  [prefix(): gathered = jax.tree.map(lambda a: lax.all_gather(a, axis), part)]
    slice x187 -> x0, local copies, waits for them, and re-layouts: 87.6 us -> none  [the longest x181 86.7 us: local_run(): lax.associative_scan(compose, (spread_field, weights), reverse=reverse, a...]
    psum x2 -> x0, blocking collectives: 33.5 us -> none  [the longest x1 30.1 us: shards(): lax.psum((jnp.sum(gradient * (gradient - prev_gradient)), jnp.sum(prev_gr...]
    ppermute x0 -> x14, waiting for transfers between devices: none -> 20.7 us  [the longest x11 15.7 us: exchange(): lax.ppermute(message, axis, [(i, (i + d) % count) for i in range(count)])]
    pallas_call x0 -> x8, Pallas kernels: none -> 18.2 us  [the longest x1 3.17 us: shards(): call(functools.partial(fourth_kernel, members, spread, len(partials)), (f...]
    ppermute x0 -> x14, starting transfers between devices: none -> 16.5 us  [the longest x11 15 us: exchange(): lax.ppermute(message, axis, [(i, (i + d) % count) for i in range(count)])]
    scatter-add x2 -> x0, other arithmetic: 6.59 us -> none  [the longest x1 3.3 us: shards(): back_north = jnp.zeros((cell_count,), jnp.float32).at[located].add(sines...]
  transfers between devices with their start and end apart: 0 -> 14, of which waited for: 0 -> 13; matrix products, arithmetic and copies ran while one was open for 0% -> 0% of each run, Pallas kernels for 0% -> 5%
where the time goes in v1:
time: 60.8 us; the launch traced here: 60.5 us
  waiting for transfers between devices  20.7 us (34%)
  Pallas kernels  18.2 us (30%)
  starting transfers between devices  16.5 us (27%)
  local copies, waits for them, and re-layouts  3.63 us (6%)
  other arithmetic  0.73 us (1%)
  between operations  0.68 us (1%)
    ppermute x11, waiting for transfers between devices, exchange(): lax.ppermute(message, axis, [(i, (i + d) % count) for i in range(count)])  15.7 us
    ppermute x11, starting transfers between devices, exchange(): lax.ppermute(message, axis, [(i, (i + d) % count) for i in range(count)])  15 us
    ppermute x2, waiting for transfers between devices, add_over(): return values + lax.ppermute(values, axis, [(0, 1), (1, 0)])  3.64 us
    unnamed x26, local copies, waits for them, and re-layouts  3.63 us
    pallas_call x1, Pallas kernels, shards(): call(functools.partial(fourth_kernel, members, spread, len(partials)), (f...  3.17 us
    pallas_call x1, Pallas kernels, shards(): call(functools.partial(second_kernel, members, n_gx), (f32(*field), f32(r...  2.84 us
    pallas_call x1, Pallas kernels, shards(): call(tables_kernel, (f32(depth, rows, columns), f32(depth, rows, columns)...  2.73 us
    pallas_call x1, Pallas kernels, shards(): call(functools.partial(fifth_kernel, members, n_gy), (f32(*extended), f32...  2 us
  transfers between devices with their start and end apart: 14, of which 13 were waited for; matrix products, arithmetic and copies ran while one was open for 0% of the time, Pallas kernels for 5%

profile of v1, /device:TPU:0, one launch (start us, length us, event | category | flops | bytes accessed | tf_op | source)
XLA Modules:
  0.0 60.5 jit_solution(4359185749707153987)
XLA Ops:
  0.6 1.8 %shard_map.121 = (f32[22,8,256]{2,1,0:T(8,128)}, f32[48,256]{1,0:T(8,128)}) custom-call(f32[20,8,256]{2,1,0:T(8,128)} %refs_6_.1, f32[8,256]{1,0:T(8,128)} %refs_5_.6), custom_call_target="tpu_custom_call" | custom-call | flops 100000 | bytes 100000 | tf_op jit(solution)/shard_map/pallas_call | solution.py:372
  2.4 5.1 %collective-permute-start.2 = (f32[48,256]{1,0:T(8,128)}, f32[48,256]{1,0:T(8,128)S(1)}, u32[]{:S(2)}, u32[]{:S(2)}) collective-permute-start(f32[48,256]{1,0:T(8,128)} %get-tuple-element.20.refs_0_), channel_id=1, source_target_pairs={{0,12},{4,0},{8,4},{12,8},{1,13},{5,1},{9,5},{13,9},{2,14},{6,2},{... | collective-permute-start | bytes 147464 | tf_op jit(solution)/shard_map/ppermute | solution.py:339
  7.5 0.0 collective-permute-start.1
  7.5 1.0 %collective-permute-start = (f32[48,256]{1,0:T(8,128)}, f32[48,256]{1,0:T(8,128)S(1)}, u32[]{:S(2)}, u32[]{:S(2)}) collective-permute-start(f32[48,256]{1,0:T(8,128)} %get-tuple-element.20.refs_0_), channel_id=1, source_target_pairs={{0,4},{4,8},{8,12},{12,0},{1,5},{5,9},{9,13},{13,1},{2,6},{6,10},{... | collective-permute-start | bytes 147464 | tf_op jit(solution)/shard_map/ppermute | solution.py:339
  8.5 2.7 %shard_map.122 = (f32[8,8,256]{2,1,0:T(8,128)}, f32[8,8,256]{2,1,0:T(8,128)}, f32[3,8,256]{2,1,0:T(8,128)}, bf16[256,512]{1,0:T(8,128)(2,1)}, f32[16,512]{1,0:T(8,128)}, /*index=5*/f32[8,256]{1,0:T(8,128)}) custom-call(f32[8,256]{1,0:T(8,128)} %refs_4_.3, s32[1,512]{1,0:T(1,128)} %bitcast.5, s32[1,512]{1,0:T(1,128)} %bitcast.6, f32[20,8,256]{2,1,0:T(8,128)} %refs_7_.3), custom_call_target="tpu_custom_call" | custom-call | flops 100000 | bytes 100000 | tf_op jit(solution)/shard_map/pallas_call | solution.py:376
  11.2 0.0 collective-permute-done.2.refs_3_
  11.2 0.0 copy-start.1
  11.2 1.4 %collective-permute-done.1.refs_2_ = f32[48,256]{1,0:T(8,128)S(1)} collective-permute-done((f32[48,256]{1,0:T(8,128)}, f32[48,256]{1,0:T(8,128)S(1)}, u32[]{:S(2)}, u32[]{:S(2)}) %collective-permute-start.1) | collective-permute-done | bytes 49184 | tf_op jit(solution)/shard_map/ppermute | solution.py:339
  12.7 0.0 copy-start.2
  12.7 0.9 %collective-permute-done.refs_1_ = f32[48,256]{1,0:T(8,128)S(1)} collective-permute-done((f32[48,256]{1,0:T(8,128)}, f32[48,256]{1,0:T(8,128)S(1)}, u32[]{:S(2)}, u32[]{:S(2)}) %collective-permute-start) | collective-permute-done | bytes 49184 | tf_op jit(solution)/shard_map/ppermute | solution.py:339
  13.6 0.0 copy-start.4
  13.6 0.0 copy-done.1
  13.6 0.0 copy-done.2
  13.6 0.6 %copy-done.4 = f32[48,256]{1,0:T(8,128)} copy-done((f32[48,256]{1,0:T(8,128)}, f32[48,256]{1,0:T(8,128)S(1)}, u32[]{:S(2)}) %copy-start.4) | copy-done | bytes 49176
  14.2 2.8 %shard_map.123 = (f32[20,8,256]{2,1,0:T(8,128)}, f32[8,128]{1,0:T(8,128)}) custom-call(f32[48,256]{1,0:T(8,128)} %get-tuple-element.20.refs_0_, f32[48,256]{1,0:T(8,128)} %copy-done.4, f32[48,256]{1,0:T(8,128)} %copy-done.2, f32[48,256]{1,0:T(8,128)} %copy-done.1, f32[22,8,256]{2,1,0:T(8,128)} %get-tuple-element.21.refs_4_, f32[8,256]{1,0:T(8,128)} %refs_4_.3, ...), custom_call_target="tpu_custom_call" | custom-call | flops 100000 | bytes 100000 | tf_op jit(solution)/shard_map/pallas_call | solution.py:387
  17.0 1.5 %collective-permute-start.3 = (f32[8,128]{1,0:T(8,128)}, f32[8,128]{1,0:T(8,128)S(1)}, u32[]{:S(2)}, u32[]{:S(2)}) collective-permute-start(f32[8,128]{1,0:T(8,128)} %get-tuple-element.25.refs_0_), channel_id=1, source_target_pairs={{0,2},{2,0},{1,3},{3,1},{4,6},{6,4},{5,7},{7,5},{8,10},{10,8},{9,1... | collective-permute-start | bytes 12296 | tf_op jit(solution)/shard_map/ppermute | solution.py:339
  18.5 2.3 %collective-permute-done.3.refs_1_ = f32[8,128]{1,0:T(8,128)S(1)} collective-permute-done((f32[8,128]{1,0:T(8,128)}, f32[8,128]{1,0:T(8,128)S(1)}, u32[]{:S(2)}, u32[]{:S(2)}) %collective-permute-start.3) | collective-permute-done | bytes 4128 | tf_op jit(solution)/shard_map/ppermute | solution.py:339
  20.9 0.0 copy-start.11
  20.9 0.6 copy-done.11
  21.4 1.9 %shard_map.124.refs_0_ = f32[16,256]{1,0:T(8,128)} custom-call(f32[8,128]{1,0:T(8,128)} %get-tuple-element.25.refs_0_, f32[8,128]{1,0:T(8,128)} %copy-done.11, f32[20,8,256]{2,1,0:T(8,128)} %get-tuple-element.26.refs_2_, f32[3,8,256]{2,1,0:T(8,128)} %get-tuple-element.24.refs_8_.refs_3_.refs_10_, bf16[2,20,8,256]{3,2,1,0:T(8,128)(2,1)} %refs_2_.1), custom_call_target="tpu_custom_call" | custom-call | flops 100000 | bytes 100000 | tf_op jit(solution)/shard_map/pallas_call | solution.py:392
  23.3 0.0 collective-permute-start.4
  23.3 1.4 %collective-permute-done.4.refs_1_ = f32[16,256]{1,0:T(8,128)S(1)} collective-permute-done((f32[16,256]{1,0:T(8,128)}, f32[16,256]{1,0:T(8,128)S(1)}, u32[]{:S(2)}, u32[]{:S(2)}) %collective-permute-start.4) | collective-permute-done | bytes 16416 | tf_op jit(solution)/shard_map/ppermute | solution.py:396
  24.7 0.0 copy-start.10
  24.7 0.6 copy-done.10
  25.3 3.2 %shard_map.125 = (f32[16,256]{1,0:T(8,128)}, f32[20,8,256]{2,1,0:T(8,128)}, f32[8,128]{1,0:T(8,128)}) custom-call(f32[16,256]{1,0:T(8,128)} %shard_map.124.refs_0_, f32[16,256]{1,0:T(8,128)} %copy-done.10, bf16[2,20,8,256]{3,2,1,0:T(8,128)(2,1)} %refs_2_.1, bf16[256,512]{1,0:T(8,128)(2,1)} %get-tuple-element.27.refs_3_, ...), custom_call_target="tpu_custom_call" | custom-call | flops 100000 | bytes 100000 | tf_op jit(solution)/shard_map/pallas_call | solution.py:399
  28.5 1.5 %collective-permute-start.5 = (f32[8,128]{1,0:T(8,128)}, f32[8,128]{1,0:T(8,128)S(1)}, u32[]{:S(2)}, u32[]{:S(2)}) collective-permute-start(f32[8,128]{1,0:T(8,128)} %get-tuple-element.29.refs_0_), channel_id=1, source_target_pairs={{0,2},{2,0},{1,3},{3,1},{4,6},{6,4},{5,7},{7,5},{8,10},{10,8},{9,1... | collective-permute-start | bytes 12296 | tf_op jit(solution)/shard_map/ppermute | solution.py:339
  30.0 2.3 %collective-permute-done.5.refs_1_ = f32[8,128]{1,0:T(8,128)S(1)} collective-permute-done((f32[8,128]{1,0:T(8,128)}, f32[8,128]{1,0:T(8,128)S(1)}, u32[]{:S(2)}, u32[]{:S(2)}) %collective-permute-start.5) | collective-permute-done | bytes 4128 | tf_op jit(solution)/shard_map/ppermute | solution.py:339
  32.3 0.0 copy-start.12
  32.3 0.6 copy-done.12
  32.9 2.0 %shard_map.126 = (f32[22,8,256]{2,1,0:T(8,128)}, f32[48,256]{1,0:T(8,128)}) custom-call(f32[8,128]{1,0:T(8,128)} %get-tuple-element.29.refs_0_, f32[8,128]{1,0:T(8,128)} %copy-done.12, f32[20,8,256]{2,1,0:T(8,128)} %get-tuple-element.30.refs_2_, f32[3,8,256]{2,1,0:T(8,128)} %get-tuple-element.24.refs_8_.refs_3_.refs_10_, f32[8,256]{1,0:T(8,128)} %refs_4_.3, ...), custom_call_target="tpu_custom_call" | custom-call | flops 100000 | bytes 100000 | tf_op jit(solution)/shard_map/pallas_call | solution.py:414
  34.9 1.3 %collective-permute-start.8 = (f32[48,256]{1,0:T(8,128)}, f32[48,256]{1,0:T(8,128)S(1)}, u32[]{:S(2)}, u32[]{:S(2)}) collective-permute-start(f32[48,256]{1,0:T(8,128)} %get-tuple-element.31.refs_0_), channel_id=1, source_target_pairs={{0,12},{4,0},{8,4},{12,8},{1,13},{5,1},{9,5},{13,9},{2,14},{6,2},{... | collective-permute-start | bytes 147464 | tf_op jit(solution)/shard_map/ppermute | solution.py:339
  36.2 0.4 collective-permute-start.7
  36.5 1.5 %collective-permute-start.6 = (f32[48,256]{1,0:T(8,128)}, f32[48,256]{1,0:T(8,128)S(1)}, u32[]{:S(2)}, u32[]{:S(2)}) collective-permute-start(f32[48,256]{1,0:T(8,128)} %get-tuple-element.31.refs_0_), channel_id=1, source_target_pairs={{0,4},{4,8},{8,12},{12,0},{1,5},{5,9},{9,13},{13,1},{2,6},{6,10},{... | collective-permute-start | bytes 147464 | tf_op jit(solution)/shard_map/ppermute | solution.py:339
  38.1 1.3 %collective-permute-done.8.refs_3_ = f32[48,256]{1,0:T(8,128)S(1)} collective-permute-done((f32[48,256]{1,0:T(8,128)}, f32[48,256]{1,0:T(8,128)S(1)}, u32[]{:S(2)}, u32[]{:S(2)}) %collective-permute-start.8) | collective-permute-done | bytes 49184 | tf_op jit(solution)/shard_map/ppermute | solution.py:339
  39.3 0.0 copy-start.3
  39.3 2.6 %collective-permute-done.7.refs_2_ = f32[48,256]{1,0:T(8,128)S(1)} collective-permute-done((f32[48,256]{1,0:T(8,128)}, f32[48,256]{1,0:T(8,128)S(1)}, u32[]{:S(2)}, u32[]{:S(2)}) %collective-permute-start.7) | collective-permute-done | bytes 49184 | tf_op jit(solution)/shard_map/ppermute | solution.py:339
  41.9 0.0 copy-start.5
  41.9 0.7 %collective-permute-done.6.refs_1_ = f32[48,256]{1,0:T(8,128)S(1)} collective-permute-done((f32[48,256]{1,0:T(8,128)}, f32[48,256]{1,0:T(8,128)S(1)}, u32[]{:S(2)}, u32[]{:S(2)}) %collective-permute-start.6) | collective-permute-done | bytes 49184 | tf_op jit(solution)/shard_map/ppermute | solution.py:339
  42.6 0.0 copy-start.6
  42.6 0.0 copy-done.3
  42.6 0.0 copy-done.5
  42.6 0.6 %copy-done.6 = f32[48,256]{1,0:T(8,128)} copy-done((f32[48,256]{1,0:T(8,128)}, f32[48,256]{1,0:T(8,128)S(1)}, u32[]{:S(2)}) %copy-start.6) | copy-done | bytes 49176
  43.3 2.0 %shard_map.127 = (f32[20,8,256]{2,1,0:T(8,128)}, f32[16,256]{1,0:T(8,128)}) custom-call(f32[48,256]{1,0:T(8,128)} %get-tuple-element.31.refs_0_, f32[48,256]{1,0:T(8,128)} %copy-done.6, f32[48,256]{1,0:T(8,128)} %copy-done.5, f32[48,256]{1,0:T(8,128)} %copy-done.3, f32[22,8,256]{2,1,0:T(8,128)} %get-tuple-element.32.refs_4_, f32[8,256]{1,0:T(8,128)} %refs_5_.6, ...), custom_call_target="tpu_custom_call" | custom-call | flops 100000 | bytes 100000 | tf_op jit(solution)/shard_map/pallas_call | solution.py:418
  45.2 0.0 collective-permute-start.9
  45.2 1.4 %collective-permute-done.9 = f32[16,256]{1,0:T(8,128)S(1)} collective-permute-done((f32[16,256]{1,0:T(8,128)}, f32[16,256]{1,0:T(8,128)S(1)}, u32[]{:S(2)}, u32[]{:S(2)}) %collective-permute-start.9) | collective-permute-done | bytes 16416 | tf_op jit(solution)/shard_map/ppermute | solution.py:345
  46.6 0.7 %add.6 = f32[16,256]{1,0:T(8,128)S(1)} add(f32[16,256]{1,0:T(8,128)} %get-tuple-element.35, f32[16,256]{1,0:T(8,128)S(1)} %collective-permute-done.9) | non-fusion elementwise | flops 4096 | bytes 49152 | tf_op jit(solution)/shard_map/add | solution.py:345
  47.3 1.5 %collective-permute-start.10 = (f32[16,256]{1,0:T(8,128)S(1)}, f32[16,256]{1,0:T(8,128)S(1)}, u32[]{:S(2)}, u32[]{:S(2)}) collective-permute-start(f32[16,256]{1,0:T(8,128)S(1)} %add.6), channel_id=1, source_target_pairs={{0,2},{2,0},{1,3},{3,1},{4,6},{6,4},{5,7},{7,5},{8,10},{10,8},{9,1... | collective-permute-start | bytes 49160 | tf_op jit(solution)/shard_map/ppermute | solution.py:345
  48.8 2.2 %collective-permute-done.10 = f32[16,256]{1,0:T(8,128)S(1)} collective-permute-done((f32[16,256]{1,0:T(8,128)S(1)}, f32[16,256]{1,0:T(8,128)S(1)}, u32[]{:S(2)}, u32[]{:S(2)}) %collective-permute-start.10) | collective-permute-done | bytes 16416 | tf_op jit(solution)/shard_map/ppermute | solution.py:345
  51.1 0.0 copy-start
  51.1 1.4 %collective-permute-start.13 = (f32[16,256]{1,0:T(8,128)S(1)}, f32[16,256]{1,0:T(8,128)S(1)}, u32[]{:S(2)}, u32[]{:S(2)}) collective-permute-start(f32[16,256]{1,0:T(8,128)S(1)} %add.7.refs_0_), channel_id=1, source_target_pairs={{0,12},{4,0},{8,4},{12,8},{1,13},{5,1},{9,5},{13,9},{2,14},{6,2},{... | collective-permute-start | bytes 49160 | tf_op jit(solution)/shard_map/ppermute | solution.py:339
  52.5 0.0 collective-permute-start.12
  52.5 1.4 %collective-permute-start.11 = (f32[16,256]{1,0:T(8,128)S(1)}, f32[16,256]{1,0:T(8,128)S(1)}, u32[]{:S(2)}, u32[]{:S(2)}) collective-permute-start(f32[16,256]{1,0:T(8,128)S(1)} %add.7.refs_0_), channel_id=1, source_target_pairs={{0,4},{4,8},{8,12},{12,0},{1,5},{5,9},{9,13},{13,1},{2,6},{6,10},{... | collective-permute-start | bytes 49160 | tf_op jit(solution)/shard_map/ppermute | solution.py:339
  53.9 1.1 %collective-permute-done.13.refs_3_ = f32[16,256]{1,0:T(8,128)S(1)} collective-permute-done((f32[16,256]{1,0:T(8,128)S(1)}, f32[16,256]{1,0:T(8,128)S(1)}, u32[]{:S(2)}, u32[]{:S(2)}) %collective-permute-start.13) | collective-permute-done | bytes 16416 | tf_op jit(solution)/shard_map/ppermute | solution.py:339
  55.0 0.0 copy-start.7
  55.0 2.1 %collective-permute-done.12.refs_2_ = f32[16,256]{1,0:T(8,128)S(1)} collective-permute-done((f32[16,256]{1,0:T(8,128)S(1)}, f32[16,256]{1,0:T(8,128)S(1)}, u32[]{:S(2)}, u32[]{:S(2)}) %collective-permute-start.12) | collective-permute-done | bytes 16416 | tf_op jit(solution)/shard_map/ppermute | solution.py:339
  57.1 0.0 copy-start.8
  57.1 0.9 %collective-permute-done.11.refs_1_ = f32[16,256]{1,0:T(8,128)S(1)} collective-permute-done((f32[16,256]{1,0:T(8,128)S(1)}, f32[16,256]{1,0:T(8,128)S(1)}, u32[]{:S(2)}, u32[]{:S(2)}) %collective-permute-start.11) | collective-permute-done | bytes 16416 | tf_op jit(solution)/shard_map/ppermute | solution.py:339
  58.0 0.0 copy-start.9
  58.0 0.0 copy-done
  58.0 0.0 copy-done.7
  58.0 0.0 copy-done.8
  58.0 0.6 copy-done.9
  58.6 1.9 %shard_map.128 = f32[20,8,256]{2,1,0:T(8,128)} custom-call(f32[16,256]{1,0:T(8,128)} %copy-done, f32[16,256]{1,0:T(8,128)} %copy-done.9, f32[16,256]{1,0:T(8,128)} %copy-done.8, f32[16,256]{1,0:T(8,128)} %copy-done.7, f32[20,8,256]{2,1,0:T(8,128)} %get-tuple-element.17.refs_4_, f32[20,8,256]{2,1,0:T(8,128)} %refs_5_.7), custom_call_target="tpu_custom_call" | custom-call | flops 100000 | bytes 100000 | tf_op jit(solution)/shard_map/pallas_call | solution.py:425
  (1 shorter events, 0.0 us)
Async XLA Ops:
  2.4 8.8 %collective-permute-start.2 = (f32[48,256]{1,0:T(8,128)}, f32[48,256]{1,0:T(8,128)S(1)}, u32[]{:S(2)}, u32[]{:S(2)}) collective-permute-start(f32[48,256]{1,0:T(8,128)} %get-tuple-element.20.refs_0_), channel_id=1, source_target_pairs={{0,12},{4,0},{8,4},{12,8},{1,13},{5,1},{9,5},{13,9},{2,14},{6,2},{... | collective-permute-start | bytes 147464 | tf_op jit(solution)/shard_map/ppermute | solution.py:339
  7.5 5.2 %collective-permute-start.1 = (f32[48,256]{1,0:T(8,128)}, f32[48,256]{1,0:T(8,128)S(1)}, u32[]{:S(2)}, u32[]{:S(2)}) collective-permute-start(f32[48,256]{1,0:T(8,128)} %get-tuple-element.20.refs_0_), channel_id=1, source_target_pairs={{0,8},{4,12},{8,0},{12,4},{1,9},{5,13},{9,1},{13,5},{2,10},{6,14},... | collective-permute-start | bytes 147464 | tf_op jit(solution)/shard_map/ppermute | solution.py:339
  7.5 6.1 %collective-permute-start = (f32[48,256]{1,0:T(8,128)}, f32[48,256]{1,0:T(8,128)S(1)}, u32[]{:S(2)}, u32[]{:S(2)}) collective-permute-start(f32[48,256]{1,0:T(8,128)} %get-tuple-element.20.refs_0_), channel_id=1, source_target_pairs={{0,4},{4,8},{8,12},{12,0},{1,5},{5,9},{9,13},{13,1},{2,6},{6,10},{... | collective-permute-start | bytes 147464 | tf_op jit(solution)/shard_map/ppermute | solution.py:339
  11.2 2.4 %copy-start.1 = (f32[48,256]{1,0:T(8,128)}, f32[48,256]{1,0:T(8,128)S(1)}, u32[]{:S(2)}) copy-start(f32[48,256]{1,0:T(8,128)S(1)} %collective-permute-done.2.refs_3_) | copy-start | bytes 147460
  12.7 0.9 %copy-start.2 = (f32[48,256]{1,0:T(8,128)}, f32[48,256]{1,0:T(8,128)S(1)}, u32[]{:S(2)}) copy-start(f32[48,256]{1,0:T(8,128)S(1)} %collective-permute-done.1.refs_2_) | copy-start | bytes 147460
  13.6 0.6 %copy-start.4 = (f32[48,256]{1,0:T(8,128)}, f32[48,256]{1,0:T(8,128)S(1)}, u32[]{:S(2)}) copy-start(f32[48,256]{1,0:T(8,128)S(1)} %collective-permute-done.refs_1_) | copy-start | bytes 147460
  17.0 3.8 %collective-permute-start.3 = (f32[8,128]{1,0:T(8,128)}, f32[8,128]{1,0:T(8,128)S(1)}, u32[]{:S(2)}, u32[]{:S(2)}) collective-permute-start(f32[8,128]{1,0:T(8,128)} %get-tuple-element.25.refs_0_), channel_id=1, source_target_pairs={{0,2},{2,0},{1,3},{3,1},{4,6},{6,4},{5,7},{7,5},{8,10},{10,8},{9,1... | collective-permute-start | bytes 12296 | tf_op jit(solution)/shard_map/ppermute | solution.py:339
  20.9 0.6 copy-start.11
  23.3 1.4 %collective-permute-start.4 = (f32[16,256]{1,0:T(8,128)}, f32[16,256]{1,0:T(8,128)S(1)}, u32[]{:S(2)}, u32[]{:S(2)}) collective-permute-start(f32[16,256]{1,0:T(8,128)} %shard_map.124.refs_0_), channel_id=1, source_target_pairs={{0,1},{1,0},{2,3},{3,2},{4,5},{5,4},{6,7},{7,6},{8,9},{9,8},{10,11... | collective-permute-start | bytes 49160 | tf_op jit(solution)/shard_map/ppermute | solution.py:396
  24.7 0.6 copy-start.10
  28.5 3.8 %collective-permute-start.5 = (f32[8,128]{1,0:T(8,128)}, f32[8,128]{1,0:T(8,128)S(1)}, u32[]{:S(2)}, u32[]{:S(2)}) collective-permute-start(f32[8,128]{1,0:T(8,128)} %get-tuple-element.29.refs_0_), channel_id=1, source_target_pairs={{0,2},{2,0},{1,3},{3,1},{4,6},{6,4},{5,7},{7,5},{8,10},{10,8},{9,1... | collective-permute-start | bytes 12296 | tf_op jit(solution)/shard_map/ppermute | solution.py:339
  32.3 0.6 copy-start.12
  34.9 4.4 %collective-permute-start.8 = (f32[48,256]{1,0:T(8,128)}, f32[48,256]{1,0:T(8,128)S(1)}, u32[]{:S(2)}, u32[]{:S(2)}) collective-permute-start(f32[48,256]{1,0:T(8,128)} %get-tuple-element.31.refs_0_), channel_id=1, source_target_pairs={{0,12},{4,0},{8,4},{12,8},{1,13},{5,1},{9,5},{13,9},{2,14},{6,2},{... | collective-permute-start | bytes 147464 | tf_op jit(solution)/shard_map/ppermute | solution.py:339
  36.2 5.7 %collective-permute-start.7 = (f32[48,256]{1,0:T(8,128)}, f32[48,256]{1,0:T(8,128)S(1)}, u32[]{:S(2)}, u32[]{:S(2)}) collective-permute-start(f32[48,256]{1,0:T(8,128)} %get-tuple-element.31.refs_0_), channel_id=1, source_target_pairs={{0,8},{4,12},{8,0},{12,4},{1,9},{5,13},{9,1},{13,5},{2,10},{6,14},... | collective-permute-start | bytes 147464 | tf_op jit(solution)/shard_map/ppermute | solution.py:339
  36.5 6.1 %collective-permute-start.6 = (f32[48,256]{1,0:T(8,128)}, f32[48,256]{1,0:T(8,128)S(1)}, u32[]{:S(2)}, u32[]{:S(2)}) collective-permute-start(f32[48,256]{1,0:T(8,128)} %get-tuple-element.31.refs_0_), channel_id=1, source_target_pairs={{0,4},{4,8},{8,12},{12,0},{1,5},{5,9},{9,13},{13,1},{2,6},{6,10},{... | collective-permute-start | bytes 147464 | tf_op jit(solution)/shard_map/ppermute | solution.py:339
  39.3 3.3 %copy-start.3 = (f32[48,256]{1,0:T(8,128)}, f32[48,256]{1,0:T(8,128)S(1)}, u32[]{:S(2)}) copy-start(f32[48,256]{1,0:T(8,128)S(1)} %collective-permute-done.8.refs_3_) | copy-start | bytes 147460
  41.9 0.7 %copy-start.5 = (f32[48,256]{1,0:T(8,128)}, f32[48,256]{1,0:T(8,128)S(1)}, u32[]{:S(2)}) copy-start(f32[48,256]{1,0:T(8,128)S(1)} %collective-permute-done.7.refs_2_) | copy-start | bytes 147460
  42.6 0.6 %copy-start.6 = (f32[48,256]{1,0:T(8,128)}, f32[48,256]{1,0:T(8,128)S(1)}, u32[]{:S(2)}) copy-start(f32[48,256]{1,0:T(8,128)S(1)} %collective-permute-done.6.refs_1_) | copy-start | bytes 147460
  45.2 1.4 %collective-permute-start.9 = (f32[16,256]{1,0:T(8,128)}, f32[16,256]{1,0:T(8,128)S(1)}, u32[]{:S(2)}, u32[]{:S(2)}) collective-permute-start(f32[16,256]{1,0:T(8,128)} %get-tuple-element.35), channel_id=1, source_target_pairs={{0,1},{1,0},{2,3},{3,2},{4,5},{5,4},{6,7},{7,6},{8,9},{9,8},{10,11... | collective-permute-start | bytes 49160 | tf_op jit(solution)/shard_map/ppermute | solution.py:345
  47.3 3.7 %collective-permute-start.10 = (f32[16,256]{1,0:T(8,128)S(1)}, f32[16,256]{1,0:T(8,128)S(1)}, u32[]{:S(2)}, u32[]{:S(2)}) collective-permute-start(f32[16,256]{1,0:T(8,128)S(1)} %add.6), channel_id=1, source_target_pairs={{0,2},{2,0},{1,3},{3,1},{4,6},{6,4},{5,7},{7,5},{8,10},{10,8},{9,1... | collective-permute-start | bytes 49160 | tf_op jit(solution)/shard_map/ppermute | solution.py:345
  51.1 6.9 %copy-start = (f32[16,256]{1,0:T(8,128)}, f32[16,256]{1,0:T(8,128)S(1)}, u32[]{:S(2)}) copy-start(f32[16,256]{1,0:T(8,128)S(1)} %add.7.refs_0_) | copy-start | bytes 49156
  51.1 3.9 %collective-permute-start.13 = (f32[16,256]{1,0:T(8,128)S(1)}, f32[16,256]{1,0:T(8,128)S(1)}, u32[]{:S(2)}, u32[]{:S(2)}) collective-permute-start(f32[16,256]{1,0:T(8,128)S(1)} %add.7.refs_0_), channel_id=1, source_target_pairs={{0,12},{4,0},{8,4},{12,8},{1,13},{5,1},{9,5},{13,9},{2,14},{6,2},{... | collective-permute-start | bytes 49160 | tf_op jit(solution)/shard_map/ppermute | solution.py:339
  52.5 4.6 %collective-permute-start.12 = (f32[16,256]{1,0:T(8,128)S(1)}, f32[16,256]{1,0:T(8,128)S(1)}, u32[]{:S(2)}, u32[]{:S(2)}) collective-permute-start(f32[16,256]{1,0:T(8,128)S(1)} %add.7.refs_0_), channel_id=1, source_target_pairs={{0,8},{4,12},{8,0},{12,4},{1,9},{5,13},{9,1},{13,5},{2,10},{6,14},... | collective-permute-start | bytes 49160 | tf_op jit(solution)/shard_map/ppermute | solution.py:339
  52.5 5.5 %collective-permute-start.11 = (f32[16,256]{1,0:T(8,128)S(1)}, f32[16,256]{1,0:T(8,128)S(1)}, u32[]{:S(2)}, u32[]{:S(2)}) collective-permute-start(f32[16,256]{1,0:T(8,128)S(1)} %add.7.refs_0_), channel_id=1, source_target_pairs={{0,4},{4,8},{8,12},{12,0},{1,5},{5,9},{9,13},{13,1},{2,6},{6,10},{... | collective-permute-start | bytes 49160 | tf_op jit(solution)/shard_map/ppermute | solution.py:339
  55.0 3.0 %copy-start.7 = (f32[16,256]{1,0:T(8,128)}, f32[16,256]{1,0:T(8,128)S(1)}, u32[]{:S(2)}) copy-start(f32[16,256]{1,0:T(8,128)S(1)} %collective-permute-done.13.refs_3_) | copy-start | bytes 49156
  57.1 0.9 %copy-start.8 = (f32[16,256]{1,0:T(8,128)}, f32[16,256]{1,0:T(8,128)S(1)}, u32[]{:S(2)}) copy-start(f32[16,256]{1,0:T(8,128)S(1)} %collective-permute-done.12.refs_2_) | copy-start | bytes 49156
  58.0 0.6 %copy-start.9 = (f32[16,256]{1,0:T(8,128)}, f32[16,256]{1,0:T(8,128)S(1)}, u32[]{:S(2)}) copy-start(f32[16,256]{1,0:T(8,128)S(1)} %collective-permute-done.11.refs_1_) | copy-start | bytes 49156

commit v2 on v1

--- a/solution.py
+++ b/solution.py
@@ -11,13 +11,17 @@
 NDIR = 72
 SUB = 8
 LANES = 128
+LIMIT = 8 * 2**20
 VMEM_SPEC = pl.BlockSpec(memory_space=pltpu.VMEM)
-
-
-def call(body, out_shape, scratch=(), flops=100000, moved=100000):
+HBM_SPEC = pl.BlockSpec(memory_space=pltpu.HBM)
+
+
+def call(body, out_shape, scratch=(), flops=100000, moved=100000, **specs):
     return pl.pallas_call(
         body,
         out_shape=out_shape,
+        **specs,
+        compiler_params=pltpu.CompilerParams(vmem_limit_bytes=LIMIT),
         scratch_shapes=list(scratch),
         cost_estimate=pl.CostEstimate(flops=flops, bytes_accessed=moved, transcendentals=0),
     )
@@ -173,14 +177,33 @@
     return [ref[n] for n in range(ref.shape[0])]
 
 
-def first_kernel(members, controls_ref, rates_ref, local_ref, message_ref):
+def first_kernel(members, far_controls_ref, far_rates_ref, local_ref, message_ref, controls_ref, rates_ref, semaphores):
+    fetches = (
+        pltpu.make_async_copy(far_rates_ref, rates_ref, semaphores.at[0]),
+        pltpu.make_async_copy(far_controls_ref, controls_ref, semaphores.at[1]),
+    )
+    for fetch in fetches:
+        fetch.start()
+    for fetch in fetches:
+        fetch.wait()
     rates = rates_ref[...]
     scales = jnp.sqrt(1.0 - rates * rates)
     x_sweeps(lambda k: scales * controls_ref[k], members, rates, scales, storer(local_ref), message_ref)
 
 
 def tables_kernel(
-    rates_ref, cells_ref, codes_ref, old_ref, forward_ref, reverse_ref, response_ref, columns_ref, weights_ref, old_sum_ref
+    rates_ref,
+    cells_ref,
+    codes_ref,
+    values_ref,
+    precisions_ref,
+    old_ref,
+    forward_ref,
+    reverse_ref,
+    response_ref,
+    columns_ref,
+    weights_ref,
+    old_sum_ref,
 ):
     rates = rates_ref[...]
     rows, columns = rates.shape
@@ -198,7 +221,9 @@
     bearing = codes_ref[...].astype(jnp.float32) * (2.0 * math.pi / NDIR)
     row = lax.broadcasted_iota(jnp.int32, (rows, count), 0) == cells // columns
     weights_ref[:rows] = jnp.where(row, jnp.cos(bearing), 0.0)
-    weights_ref[rows:] = jnp.where(row, jnp.sin(bearing), 0.0)
+    weights_ref[rows : 2 * rows] = jnp.where(row, jnp.sin(bearing), 0.0)
+    weights_ref[2 * rows : 2 * rows + 1] = values_ref[...]
+    weights_ref[2 * rows + 1 : 2 * rows + 2] = precisions_ref[...]
     total = jnp.zeros((rows, columns), jnp.float32)
     for k in range(old_ref.shape[0]):
         total += old_ref[k] * old_ref[k]
@@ -247,8 +272,6 @@
         anomalies_ref,
         columns_ref,
         weights_ref,
-        values_ref,
-        precisions_ref,
         rates_ref,
         forward_ref,
         reverse_ref,
@@ -264,9 +287,10 @@
         increment = increment + ref[...]
     increment_ref[...] = increment
     picked = split_dot(increment, columns_ref[...], ((1,), (0,)))
-    weights = weights_ref[...]
+    weights = weights_ref[: 2 * rows]
+    values, precisions = weights_ref[2 * rows : 2 * rows + 1], weights_ref[2 * rows + 1 : 2 * rows + 2]
     projected = jnp.sum(weights * picked, axis=0, keepdims=True)
-    misfit = precisions_ref[...] * (projected - values_ref[...])
+    misfit = precisions * (projected - values)
     back = split_dot(weights * misfit, columns_ref[...], ((1,), (1,)))
     scales = jnp.sqrt(1.0 - rates * rates)
     east = back[:rows] * rates * spread
@@ -312,25 +336,29 @@
         )
         gradient_ref[k] = gradient
         total += gradient * (gradient - old_ref[k])
-    sums_ref[:rows] = total
-    sums_ref[rows:] = old_sum_ref[...]
-
-
-def last_kernel(stacked, *refs):
-    sums = refs[:-3]
-    gradient_ref, old_ref, direction_ref = refs[-3:]
-    if stacked:
-        total = jnp.sum(sums[0][...], axis=0)
-    else:
-        total = sums[0][...]
-        for ref in sums[1:]:
-            total = total + ref[...]
-    half = total.shape[0] // 2
-    numerator = jnp.sum(total[:half], axis=(0, 1), keepdims=True)
-    denominator = jnp.sum(total[half:], axis=(0, 1), keepdims=True)
+    sums = (jnp.sum(total, axis=0, keepdims=True), jnp.sum(old_sum_ref[...], axis=0, keepdims=True))
+    row = lax.broadcasted_iota(jnp.int32, (SUB, columns), 0)
+    sums = jnp.where(row == 0, sums[0], jnp.where(row == 1, sums[1], 0.0))
+    packed = sums[:, :LANES]
+    for at in range(LANES, columns, LANES):
+        packed = packed + sums[:, at : at + LANES]
+    for n in range(sums_ref.shape[0]):
+        sums_ref[n] = packed
+
+
+def last_kernel(sums_ref, near_ref, old_ref, gradient_ref, far_ref, direction_ref, semaphores):
+    copies = [pltpu.make_async_copy(near_ref, gradient_ref, semaphores.at[0])]
+    copies[0].start()
+    total = jnp.sum(sums_ref[...], axis=0)
+    numerator = jnp.sum(total[:1], axis=1, keepdims=True)
+    denominator = jnp.sum(total[1:2], axis=1, keepdims=True)
     ratio = numerator / denominator
-    for k in range(gradient_ref.shape[0]):
-        direction_ref[k] = ratio * old_ref[k] - gradient_ref[k]
+    for k in range(near_ref.shape[0]):
+        direction_ref[k] = ratio * old_ref[k] - near_ref[k]
+    copies.append(pltpu.make_async_copy(direction_ref, far_ref, semaphores.at[1]))
+    copies[1].start()
+    for copy in copies:
+        copy.wait()
 
 
 def exchange(message, axis, count):
@@ -338,12 +366,6 @@
         shifts = range(1, count)
         return [message] + [lax.ppermute(message, axis, [(i, (i + d) % count) for i in range(count)]) for d in shifts]
     return [lax.all_gather(message, axis)]
-
-
-def add_over(values, axis, count):
-    if count == 2:
-        return values + lax.ppermute(values, axis, [(0, 1), (1, 0)])
-    return lax.psum(values, axis)
 
 
 def shards(
@@ -370,7 +392,9 @@
     extended = (members + 2, rows, columns)
 
     local, message = call(
-        functools.partial(first_kernel, members), (f32(*extended), f32(lines, columns))
+        functools.partial(first_kernel, members), (f32(*extended), f32(lines, columns)),
+        [pltpu.VMEM(field, jnp.float32), pltpu.VMEM((rows, columns), jnp.float32), pltpu.SemaphoreType.DMA((2,))],
+        in_specs=[HBM_SPEC, HBM_SPEC],
     )(controls, x_rates)
     x_messages = exchange(message, "gx", n_gx)
     forward, reverse, response, column_ones, row_weights, old_sum = call(
@@ -380,10 +404,17 @@
             f32(depth, rows, columns),
             f32(3, rows, columns),
             jax.ShapeDtypeStruct((columns, observed), jnp.bfloat16),
-            f32(2 * rows, observed),
+            f32(2 * rows + SUB, observed),
             f32(rows, columns),
         ),
-    )(y_rates, obs_cells.reshape(1, observed), obs_codes.reshape(1, observed), prev_gradient)
+    )(
+        y_rates,
+        obs_cells.reshape(1, observed),
+        obs_codes.reshape(1, observed),
+        obs_values.reshape(1, observed),
+        obs_weights.reshape(1, observed),
+        prev_gradient,
+    )
     filtered, message = call(
         functools.partial(second_kernel, members, n_gx),
         (f32(*field), f32(rows, LANES)),
@@ -404,8 +435,6 @@
         anomalies,
         column_ones,
         row_weights,
-        obs_values.reshape(1, observed),
-        obs_weights.reshape(1, observed),
         y_rates,
         forward,
         reverse,
@@ -417,14 +446,16 @@
     )(*exchange(message, "gy", n_gy), pulled, response, y_rates, x_rates)
     gradient, sums = call(
         functools.partial(sixth_kernel, members, n_gx),
-        (f32(*field), f32(2 * rows, columns)),
+        (f32(*field), f32(n_gx * n_gy * n_gz, SUB, LANES)),
         [pltpu.VMEM((lines, columns), jnp.float32)],
     )(*exchange(message, "gx", n_gx), local, x_rates, controls, prev_gradient, old_sum)
-    sums = add_over(add_over(sums, "gz", n_gz), "gy", n_gy)
-    totals = exchange(sums, "gx", n_gx)
-    direction = call(functools.partial(last_kernel, len(totals) != n_gx), f32(*field))(
-        *totals, gradient, prev_direction
-    )
+    sums = lax.all_to_all(sums, ("gx", "gy", "gz"), 0, 0)
+    gradient, direction = call(
+        last_kernel,
+        (f32(*field), f32(*field)),
+        [pltpu.VMEM(field, jnp.float32), pltpu.SemaphoreType.DMA((2,))],
+        out_specs=(HBM_SPEC, HBM_SPEC),
+    )(sums, gradient, prev_direction)
     return gradient, direction, increment.reshape(2, rows, columns)
 
 

time: 60.8 us -> 45 us (0.74)
  Pallas kernels: 18.2 us -> 6.05 us
  blocking collectives: 0 us -> 10.6 us
  waiting for transfers between devices: 20.7 us -> 13.4 us
  starting transfers between devices: 16.5 us -> 12.5 us
  local copies, waits for them, and re-layouts: 3.63 us -> 1.64 us
  other arithmetic: 0.73 us -> 0 us
    all_to_all x0 -> x1, blocking collectives: none -> 10.6 us  [shards(): sums = lax.all_to_all(sums, ('gx', 'gy', 'gz'), 0, 0)]
    ppermute x2 -> x0, waiting for transfers between devices: 3.64 us -> none  [add_over(): return values + lax.ppermute(values, axis, [(0, 1), (1, 0)])]
    ppermute x11 -> x8, waiting for transfers between devices: 15.7 us -> 12.2 us  [exchange(): lax.ppermute(message, axis, [(i, (i + d) % count) for i in range(count)])]
    pallas_call x2, Pallas kernels: 3.83 us -> 0.94 us  [the longest x1 0.83 us: shards(): call(last_kernel, (f32(*field), f32(*field)), [pltpu.VMEM(field, jnp.floa...]
    ppermute x11 -> x8, starting transfers between devices: 15 us -> 12.4 us  [exchange(): lax.ppermute(message, axis, [(i, (i + d) % count) for i in range(count)])]
    unnamed x26 -> x22, local copies, waits for them, and re-layouts: 3.63 us -> 1.64 us
    pallas_call x1, Pallas kernels: 2.73 us -> 1.03 us  [shards(): call(tables_kernel, (f32(depth, rows, columns), f32(depth, rows, columns)...]
    pallas_call x1, Pallas kernels: 2.84 us -> 1.16 us  [shards(): call(functools.partial(second_kernel, members, n_gx), (f32(*field), f32(r...]
  transfers between devices with their start and end apart: 14 -> 9, of which waited for: 13 -> 7; matrix products, arithmetic and copies ran while one was open for 0% -> 0% of each run, Pallas kernels for 5% -> 2%
where the time goes in v2:
time: 45 us; the launch traced here: 44.8 us
  waiting for transfers between devices  13.4 us (30%)
  starting transfers between devices  12.5 us (28%)
  blocking collectives  10.6 us (24%)
  Pallas kernels  6.05 us (13%)
  local copies, waits for them, and re-layouts  1.64 us (4%)
  between operations  0.74 us (2%)
    ppermute x8, starting transfers between devices, exchange(): lax.ppermute(message, axis, [(i, (i + d) % count) for i in range(count)])  12.4 us
    ppermute x8, waiting for transfers between devices, exchange(): lax.ppermute(message, axis, [(i, (i + d) % count) for i in range(count)])  12.2 us
    all_to_all x1, blocking collectives, shards(): sums = lax.all_to_all(sums, ('gx', 'gy', 'gz'), 0, 0)  10.6 us
    pallas_call x1, Pallas kernels, shards(): call(functools.partial(fourth_kernel, members, spread, len(partials)), (f...  1.92 us
    unnamed x22, local copies, waits for them, and re-layouts  1.64 us
    ppermute x1, waiting for transfers between devices, shards(): partials = [partial, lax.ppermute(partial, 'gz', [(0, 1), (1, 0)])]  1.17 us
    pallas_call x1, Pallas kernels, shards(): call(functools.partial(second_kernel, members, n_gx), (f32(*field), f32(r...  1.16 us
    pallas_call x1, Pallas kernels, shards(): call(tables_kernel, (f32(depth, rows, columns), f32(depth, rows, columns)...  1.03 us
  transfers between devices with their start and end apart: 9, of which 7 were waited for; matrix products, arithmetic and copies ran while one was open for 0% of the time, Pallas kernels for 2%

profile of v2, /device:TPU:0, one launch (start us, length us, event | category | flops | bytes accessed | tf_op | source)
XLA Modules:
  0.0 44.8 jit_solution(16119664371660075515)
XLA Ops:
  0.6 0.0 copy-start.1
  0.6 0.9 %copy-done.1 = f32[20,8,256]{2,1,0:T(8,128)S(1)} copy-done((f32[20,8,256]{2,1,0:T(8,128)S(1)}, f32[20,8,256]{2,1,0:T(8,128)}, u32[]{:S(2)}) %copy-start.1) | copy-done | bytes 163864
  1.6 0.0 copy-start.6
  1.6 0.7 %copy-done.6 = f32[8,256]{1,0:T(8,128)S(1)} copy-done((f32[8,256]{1,0:T(8,128)S(1)}, f32[8,256]{1,0:T(8,128)}, u32[]{:S(2)}) %copy-start.6) | copy-done | bytes 8216
  2.2 0.0 copy-start.3
  2.3 0.0 copy-start.7
  2.3 0.0 copy-start.8
  2.3 0.0 copy-start.9
  2.3 0.0 copy-start.10
  2.3 0.4 shard_map.121
  2.7 0.0 copy-start.5
  2.7 5.1 %collective-permute-start.2 = (f32[48,256]{1,0:T(8,128)S(1)}, f32[48,256]{1,0:T(8,128)S(1)}, u32[]{:S(2)}, u32[]{:S(2)}) collective-permute-start(f32[48,256]{1,0:T(8,128)S(1)} %get-tuple-element.22.refs_0_), channel_id=1, source_target_pairs={{0,12},{4,0},{8,4},{12,8},{1,13},{5,1},{9,5},{13,9},{2,14},{6,2},{... | collective-permute-start | bytes 147464 | tf_op jit(solution)/shard_map/ppermute | solution.py:367
  7.8 0.0 collective-permute-start.1
  7.8 1.0 %collective-permute-start = (f32[48,256]{1,0:T(8,128)S(1)}, f32[48,256]{1,0:T(8,128)S(1)}, u32[]{:S(2)}, u32[]{:S(2)}) collective-permute-start(f32[48,256]{1,0:T(8,128)S(1)} %get-tuple-element.22.refs_0_), channel_id=1, source_target_pairs={{0,4},{4,8},{8,12},{12,0},{1,5},{5,9},{9,13},{13,1},{2,6},{6,10},{... | collective-permute-start | bytes 147464 | tf_op jit(solution)/shard_map/ppermute | solution.py:367
  8.8 0.0 copy-done.3
  8.8 0.0 copy-done.7
  8.8 0.0 copy-done.8
  8.8 0.0 copy-done.9
  8.8 0.0 copy-done.10
  8.9 0.0 copy-done.5
  8.9 1.0 %shard_map.122 = (f32[8,8,256]{2,1,0:T(8,128)S(1)}, f32[8,8,256]{2,1,0:T(8,128)S(1)}, f32[3,8,256]{2,1,0:T(8,128)S(1)}, bf16[256,512]{1,0:T(8,128)(2,1)S(1)}, f3...) custom-call(f32[8,256]{1,0:T(8,128)S(1)} %copy-done.5, s32[1,512]{1,0:T(1,128)S(1)} %bitcast.5, s32[1,512]{1,0:T(1,128)S(1)} %bitcast.6, ...), custom_call_target="tpu_custom_call" | custom-call | flops 100000 | bytes 100000 | tf_op jit(solution)/shard_map/pallas_call | solution.py:400
  9.9 0.0 collective-permute-done.2.refs_3_
  9.9 2.9 %collective-permute-done.1.refs_2_ = f32[48,256]{1,0:T(8,128)S(1)} collective-permute-done((f32[48,256]{1,0:T(8,128)S(1)}, f32[48,256]{1,0:T(8,128)S(1)}, u32[]{:S(2)}, u32[]{:S(2)}) %collective-permute-start.1) | collective-permute-done | bytes 49184 | tf_op jit(solution)/shard_map/ppermute | solution.py:367
  12.8 0.9 %collective-permute-done.refs_1_ = f32[48,256]{1,0:T(8,128)S(1)} collective-permute-done((f32[48,256]{1,0:T(8,128)S(1)}, f32[48,256]{1,0:T(8,128)S(1)}, u32[]{:S(2)}, u32[]{:S(2)}) %collective-permute-start) | collective-permute-done | bytes 49184 | tf_op jit(solution)/shard_map/ppermute | solution.py:367
  13.7 0.0 copy-start
  13.7 1.2 %shard_map.123 = (f32[20,8,256]{2,1,0:T(8,128)S(1)}, f32[8,128]{1,0:T(8,128)S(1)}) custom-call(f32[48,256]{1,0:T(8,128)S(1)} %get-tuple-element.22.refs_0_, f32[48,256]{1,0:T(8,128)S(1)} %collective-permute-done.refs_1_, f32[48,256]{1,0:T(8,128)S(1)} %collective-permute-done.1.refs_2_, f32[48,256]{1,0:T(8,128)S(1)} %collective-permute-done.2.refs_3_, ...), custom_call_target="tpu_custom_call" | custom-call | flops 100000 | bytes 100000 | tf_op jit(solution)/shard_map/pallas_call | solution.py:418
  14.9 1.6 %collective-permute-start.3 = (f32[8,128]{1,0:T(8,128)S(1)}, f32[8,128]{1,0:T(8,128)S(1)}, u32[]{:S(2)}, u32[]{:S(2)}) collective-permute-start(f32[8,128]{1,0:T(8,128)S(1)} %get-tuple-element.27.refs_0_), channel_id=1, source_target_pairs={{0,2},{2,0},{1,3},{3,1},{4,6},{6,4},{5,7},{7,5},{8,10},{10,8},{9,1... | collective-permute-start | bytes 12296 | tf_op jit(solution)/shard_map/ppermute | solution.py:367
  16.4 2.1 %collective-permute-done.3.refs_1_ = f32[8,128]{1,0:T(8,128)S(1)} collective-permute-done((f32[8,128]{1,0:T(8,128)S(1)}, f32[8,128]{1,0:T(8,128)S(1)}, u32[]{:S(2)}, u32[]{:S(2)}) %collective-permute-start.3) | collective-permute-done | bytes 4128 | tf_op jit(solution)/shard_map/ppermute | solution.py:367
  18.5 0.0 copy-done
  18.6 0.3 shard_map.124.refs_0_
  18.8 0.1 collective-permute-start.4
  18.9 1.2 %collective-permute-done.4.refs_1_ = f32[16,256]{1,0:T(8,128)S(1)} collective-permute-done((f32[16,256]{1,0:T(8,128)S(1)}, f32[16,256]{1,0:T(8,128)S(1)}, u32[]{:S(2)}, u32[]{:S(2)}) %collective-permute-start.4) | collective-permute-done | bytes 16416 | tf_op jit(solution)/shard_map/ppermute | solution.py:427
  20.1 1.9 %shard_map.125 = (f32[16,256]{1,0:T(8,128)}, f32[20,8,256]{2,1,0:T(8,128)S(1)}, f32[8,128]{1,0:T(8,128)S(1)}) custom-call(f32[16,256]{1,0:T(8,128)S(1)} %shard_map.124.refs_0_, f32[16,256]{1,0:T(8,128)S(1)} %collective-permute-done.4.refs_1_, bf16[2,20,8,256]{3,2,1,0:T(8,128)(2,1)S(1)} %copy-done, bf16[256,512]{1,0:T(8,128)(2,1)S(1)} %get-tuple-element.29.refs_3_, ...), custom_call_target="tpu_custom_call" | custom-call | flops 100000 | bytes 100000 | tf_op jit(solution)/shard_map/pallas_call | solution.py:430
  22.0 0.0 copy-start.2
  22.0 1.5 %collective-permute-start.5 = (f32[8,128]{1,0:T(8,128)S(1)}, f32[8,128]{1,0:T(8,128)S(1)}, u32[]{:S(2)}, u32[]{:S(2)}) collective-permute-start(f32[8,128]{1,0:T(8,128)S(1)} %get-tuple-element.31.refs_0_), channel_id=1, source_target_pairs={{0,2},{2,0},{1,3},{3,1},{4,6},{6,4},{5,7},{7,5},{8,10},{10,8},{9,1... | collective-permute-start | bytes 12296 | tf_op jit(solution)/shard_map/ppermute | solution.py:367
  23.5 2.1 %collective-permute-done.5.refs_1_ = f32[8,128]{1,0:T(8,128)S(1)} collective-permute-done((f32[8,128]{1,0:T(8,128)S(1)}, f32[8,128]{1,0:T(8,128)S(1)}, u32[]{:S(2)}, u32[]{:S(2)}) %collective-permute-start.5) | collective-permute-done | bytes 4128 | tf_op jit(solution)/shard_map/ppermute | solution.py:367
  25.6 0.3 shard_map.126
  25.9 1.3 %collective-permute-start.8 = (f32[48,256]{1,0:T(8,128)S(1)}, f32[48,256]{1,0:T(8,128)S(1)}, u32[]{:S(2)}, u32[]{:S(2)}) collective-permute-start(f32[48,256]{1,0:T(8,128)S(1)} %get-tuple-element.33.refs_0_), channel_id=1, source_target_pairs={{0,12},{4,0},{8,4},{12,8},{1,13},{5,1},{9,5},{13,9},{2,14},{6,2},{... | collective-permute-start | bytes 147464 | tf_op jit(solution)/shard_map/ppermute | solution.py:367
  27.2 0.0 collective-permute-start.7
  27.3 1.9 %collective-permute-start.6 = (f32[48,256]{1,0:T(8,128)S(1)}, f32[48,256]{1,0:T(8,128)S(1)}, u32[]{:S(2)}, u32[]{:S(2)}) collective-permute-start(f32[48,256]{1,0:T(8,128)S(1)} %get-tuple-element.33.refs_0_), channel_id=1, source_target_pairs={{0,4},{4,8},{8,12},{12,0},{1,5},{5,9},{9,13},{13,1},{2,6},{6,10},{... | collective-permute-start | bytes 147464 | tf_op jit(solution)/shard_map/ppermute | solution.py:367
  29.1 1.2 %collective-permute-done.8.refs_3_ = f32[48,256]{1,0:T(8,128)S(1)} collective-permute-done((f32[48,256]{1,0:T(8,128)S(1)}, f32[48,256]{1,0:T(8,128)S(1)}, u32[]{:S(2)}, u32[]{:S(2)}) %collective-permute-start.8) | collective-permute-done | bytes 49184 | tf_op jit(solution)/shard_map/ppermute | solution.py:367
  30.3 3.0 %collective-permute-done.7.refs_2_ = f32[48,256]{1,0:T(8,128)S(1)} collective-permute-done((f32[48,256]{1,0:T(8,128)S(1)}, f32[48,256]{1,0:T(8,128)S(1)}, u32[]{:S(2)}, u32[]{:S(2)}) %collective-permute-start.7) | collective-permute-done | bytes 49184 | tf_op jit(solution)/shard_map/ppermute | solution.py:367
  33.3 0.0 collective-permute-done.6.refs_1_
  33.3 0.0 copy-done.2
  33.3 0.0 copy-start.4
  33.3 0.1 shard_map.127
  33.4 10.6 %all_to_all.5.sums_ref = f32[16,8,128]{2,1,0:T(8,128)S(1)} all-to-all(f32[16,8,128]{2,1,0:T(8,128)S(1)} %get-tuple-element.36), channel_id=1, replica_groups=mesh['grp'=2,'gx'=4,'gy'=2,'gz'=2] {'gx','gy','gz'}, dimensions={0} | all-to-all | bytes 131072 | tf_op jit(solution)/shard_map/all_to_all | solution.py:452
  44.0 0.0 copy-done.4
  44.0 0.8 %shard_map.128 = (f32[20,8,256]{2,1,0:T(8,128)}, f32[20,8,256]{2,1,0:T(8,128)}) custom-call(f32[16,8,128]{2,1,0:T(8,128)S(1)} %all_to_all.5.sums_ref, f32[20,8,256]{2,1,0:T(8,128)S(1)} %get-tuple-element.37.near_ref, f32[20,8,256]{2,1,0:T(8,128)S(1)} %copy-done.4), custom_call_target="tpu_custom_call" | custom-call | flops 100000 | bytes 100000 | tf_op jit(solution)/shard_map/pallas_call | solution.py:453
Async XLA Ops:
  0.6 0.9 %copy-start.1 = (f32[20,8,256]{2,1,0:T(8,128)S(1)}, f32[20,8,256]{2,1,0:T(8,128)}, u32[]{:S(2)}) copy-start(f32[20,8,256]{2,1,0:T(8,128)} %refs_6_.1) | copy-start | bytes 491524
  1.6 0.7 %copy-start.6 = (f32[8,256]{1,0:T(8,128)S(1)}, f32[8,256]{1,0:T(8,128)}, u32[]{:S(2)}) copy-start(f32[8,256]{1,0:T(8,128)} %refs_5_.7) | copy-start | bytes 24580
  2.2 6.6 %copy-start.3 = (f32[20,8,256]{2,1,0:T(8,128)S(1)}, f32[20,8,256]{2,1,0:T(8,128)}, u32[]{:S(2)}) copy-start(f32[20,8,256]{2,1,0:T(8,128)} %refs_7_.1) | copy-start | bytes 491524
  2.3 6.6 %copy-start.7 = (s32[1,1,512]{2,1,0:T(1,128)S(1)}, s32[1,1,512]{2,1,0:T(1,128)}, u32[]{:S(2)}) copy-start(s32[1,1,512]{2,1,0:T(1,128)} %param.14) | copy-start | bytes 6148
  2.3 6.6 %copy-start.8 = (s32[1,1,512]{2,1,0:T(1,128)S(1)}, s32[1,1,512]{2,1,0:T(1,128)}, u32[]{:S(2)}) copy-start(s32[1,1,512]{2,1,0:T(1,128)} %param.15) | copy-start | bytes 6148
  2.3 6.6 %copy-start.9 = (f32[1,1,512]{2,1,0:T(1,128)S(1)}, f32[1,1,512]{2,1,0:T(1,128)}, u32[]{:S(2)}) copy-start(f32[1,1,512]{2,1,0:T(1,128)} %param.16) | copy-start | bytes 6148
  2.3 6.6 %copy-start.10 = (f32[1,1,512]{2,1,0:T(1,128)S(1)}, f32[1,1,512]{2,1,0:T(1,128)}, u32[]{:S(2)}) copy-start(f32[1,1,512]{2,1,0:T(1,128)} %param.17) | copy-start | bytes 6148
  2.7 6.2 %copy-start.5 = (f32[8,256]{1,0:T(8,128)S(1)}, f32[8,256]{1,0:T(8,128)}, u32[]{:S(2)}) copy-start(f32[8,256]{1,0:T(8,128)} %refs_4_.3) | copy-start | bytes 24580
  2.7 7.2 %collective-permute-start.2 = (f32[48,256]{1,0:T(8,128)S(1)}, f32[48,256]{1,0:T(8,128)S(1)}, u32[]{:S(2)}, u32[]{:S(2)}) collective-permute-start(f32[48,256]{1,0:T(8,128)S(1)} %get-tuple-element.22.refs_0_), channel_id=1, source_target_pairs={{0,12},{4,0},{8,4},{12,8},{1,13},{5,1},{9,5},{13,9},{2,14},{6,2},{... | collective-permute-start | bytes 147464 | tf_op jit(solution)/shard_map/ppermute | solution.py:367
  7.8 5.0 %collective-permute-start.1 = (f32[48,256]{1,0:T(8,128)S(1)}, f32[48,256]{1,0:T(8,128)S(1)}, u32[]{:S(2)}, u32[]{:S(2)}) collective-permute-start(f32[48,256]{1,0:T(8,128)S(1)} %get-tuple-element.22.refs_0_), channel_id=1, source_target_pairs={{0,8},{4,12},{8,0},{12,4},{1,9},{5,13},{9,1},{13,5},{2,10},{6,14},... | collective-permute-start | bytes 147464 | tf_op jit(solution)/shard_map/ppermute | solution.py:367
  7.8 5.9 %collective-permute-start = (f32[48,256]{1,0:T(8,128)S(1)}, f32[48,256]{1,0:T(8,128)S(1)}, u32[]{:S(2)}, u32[]{:S(2)}) collective-permute-start(f32[48,256]{1,0:T(8,128)S(1)} %get-tuple-element.22.refs_0_), channel_id=1, source_target_pairs={{0,4},{4,8},{8,12},{12,0},{1,5},{5,9},{9,13},{13,1},{2,6},{6,10},{... | collective-permute-start | bytes 147464 | tf_op jit(solution)/shard_map/ppermute | solution.py:367
  13.7 4.8 %copy-start = (bf16[2,20,8,256]{3,2,1,0:T(8,128)(2,1)S(1)}, bf16[2,20,8,256]{3,2,1,0:T(8,128)(2,1)}, u32[]{:S(2)}) copy-start(bf16[2,20,8,256]{3,2,1,0:T(8,128)(2,1)} %refs_2_.1) | copy-start | bytes 491524
  14.9 3.7 %collective-permute-start.3 = (f32[8,128]{1,0:T(8,128)S(1)}, f32[8,128]{1,0:T(8,128)S(1)}, u32[]{:S(2)}, u32[]{:S(2)}) collective-permute-start(f32[8,128]{1,0:T(8,128)S(1)} %get-tuple-element.27.refs_0_), channel_id=1, source_target_pairs={{0,2},{2,0},{1,3},{3,1},{4,6},{6,4},{5,7},{7,5},{8,10},{10,8},{9,1... | collective-permute-start | bytes 12296 | tf_op jit(solution)/shard_map/ppermute | solution.py:367
  18.8 1.2 %collective-permute-start.4 = (f32[16,256]{1,0:T(8,128)S(1)}, f32[16,256]{1,0:T(8,128)S(1)}, u32[]{:S(2)}, u32[]{:S(2)}) collective-permute-start(f32[16,256]{1,0:T(8,128)S(1)} %shard_map.124.refs_0_), channel_id=1, source_target_pairs={{0,1},{1,0},{2,3},{3,2},{4,5},{5,4},{6,7},{7,6},{8,9},{9,8},{10,11... | collective-permute-start | bytes 49160 | tf_op jit(solution)/shard_map/ppermute | solution.py:427
  22.0 11.3 %copy-start.2 = (f32[20,8,256]{2,1,0:T(8,128)S(1)}, f32[20,8,256]{2,1,0:T(8,128)}, u32[]{:S(2)}) copy-start(f32[20,8,256]{2,1,0:T(8,128)} %refs_6_.1) | copy-start | bytes 491524
  22.0 3.6 %collective-permute-start.5 = (f32[8,128]{1,0:T(8,128)S(1)}, f32[8,128]{1,0:T(8,128)S(1)}, u32[]{:S(2)}, u32[]{:S(2)}) collective-permute-start(f32[8,128]{1,0:T(8,128)S(1)} %get-tuple-element.31.refs_0_), channel_id=1, source_target_pairs={{0,2},{2,0},{1,3},{3,1},{4,6},{6,4},{5,7},{7,5},{8,10},{10,8},{9,1... | collective-permute-start | bytes 12296 | tf_op jit(solution)/shard_map/ppermute | solution.py:367
  25.9 4.4 %collective-permute-start.8 = (f32[48,256]{1,0:T(8,128)S(1)}, f32[48,256]{1,0:T(8,128)S(1)}, u32[]{:S(2)}, u32[]{:S(2)}) collective-permute-start(f32[48,256]{1,0:T(8,128)S(1)} %get-tuple-element.33.refs_0_), channel_id=1, source_target_pairs={{0,12},{4,0},{8,4},{12,8},{1,13},{5,1},{9,5},{13,9},{2,14},{6,2},{... | collective-permute-start | bytes 147464 | tf_op jit(solution)/shard_map/ppermute | solution.py:367
  27.2 6.0 %collective-permute-start.7 = (f32[48,256]{1,0:T(8,128)S(1)}, f32[48,256]{1,0:T(8,128)S(1)}, u32[]{:S(2)}, u32[]{:S(2)}) collective-permute-start(f32[48,256]{1,0:T(8,128)S(1)} %get-tuple-element.33.refs_0_), channel_id=1, source_target_pairs={{0,8},{4,12},{8,0},{12,4},{1,9},{5,13},{9,1},{13,5},{2,10},{6,14},... | collective-permute-start | bytes 147464 | tf_op jit(solution)/shard_map/ppermute | solution.py:367
  27.3 6.0 %collective-permute-start.6 = (f32[48,256]{1,0:T(8,128)S(1)}, f32[48,256]{1,0:T(8,128)S(1)}, u32[]{:S(2)}, u32[]{:S(2)}) collective-permute-start(f32[48,256]{1,0:T(8,128)S(1)} %get-tuple-element.33.refs_0_), channel_id=1, source_target_pairs={{0,4},{4,8},{8,12},{12,0},{1,5},{5,9},{9,13},{13,1},{2,6},{6,10},{... | collective-permute-start | bytes 147464 | tf_op jit(solution)/shard_map/ppermute | solution.py:367
  33.3 10.7 %copy-start.4 = (f32[20,8,256]{2,1,0:T(8,128)S(1)}, f32[20,8,256]{2,1,0:T(8,128)}, u32[]{:S(2)}) copy-start(f32[20,8,256]{2,1,0:T(8,128)} %old_ref.3) | copy-start | bytes 491524

commit v3 on v2

v3 whole, which is shorter than its diff:
```python
import functools
import math

import jax
import jax.numpy as jnp
from jax import lax
from jax.experimental import pallas as pl
from jax.experimental.pallas import tpu as pltpu
from jax.sharding import PartitionSpec as P

NDIR = 72
SUB = 8
LANES = 128
LIMIT = 8 * 2**20
VMEM_SPEC = pl.BlockSpec(memory_space=pltpu.VMEM)
HBM_SPEC = pl.BlockSpec(memory_space=pltpu.HBM)


def call(body, out_shape, scratch=(), flops=100000, moved=100000, **specs):
    return pl.pallas_call(
        body,
        out_shape=out_shape,
        **specs,
        compiler_params=pltpu.CompilerParams(vmem_limit_bytes=LIMIT),
        scratch_shapes=list(scratch),
        cost_estimate=pl.CostEstimate(flops=flops, bytes_accessed=moved, transcendentals=0),
    )


def f32(*shape):
    return jax.ShapeDtypeStruct(shape, jnp.float32)


def row_count(members):
    return -(-(members + 4) // SUB) * SUB


def chain(get, count, place, everywhere=False):
    first = get(0)
    zero = jnp.zeros_like(first[0])
    if count == 1:
        return zero, zero, [(zero, zero)]
    low, high, low_back, high_back = {}, {}, {}, {}
    state = zero
    for d in range(count - 1, 0, -1):
        low[d] = state
        out, _, product, _ = get(d)
        state = jnp.where(place >= d, out + product * state, state)
    entering = state
    state = first[0] + first[2] * entering
    for d in range(1, count):
        high[d] = state
        if d < count - 1:
            out, _, product, _ = get(count - d)
            state = out + product * state
    state = zero
    for d in range(count - 1, 0, -1):
        high_back[d] = state
        _, out, product, response = get(count - d)
        state = jnp.where(place + d < count, out + response * high[d] + product * state, state)
    backward = state
    if not everywhere:
        return entering, backward, []
    state = first[1] + first[3] * entering + first[2] * backward
    for d in range(1, count):
        low_back[d] = state
        if d < count - 1:
            _, out, product, response = get(d)
            state = out + response * low[d] + product * state
    every = [(entering, backward)]
    for d in range(1, count):
        above = count - d
        every.append(
            (
                jnp.where(place >= d, low[d], high[above]),
                jnp.where(place >= d, low_back[d], high_back[above]),
            )
        )
    return entering, backward, every


def source_reader(refs, count, axis):
    if len(refs) == count:
        return lambda d: refs[d][...]
    place = lax.axis_index(axis)
    return lambda d: refs[0][lax.rem(place - d + count, count)]


def x_reader(refs, count, axis, members):
    read = source_reader(refs, count, axis)
    half = row_count(members)

    def get(d):
        block = read(d)
        out, back = block[:half], block[half:]
        return out, back, out[members : members + 1], back[members : members + 1]

    return get


def y_reader(refs, count, axis, members):
    read = source_reader(refs, count, axis)
    half = LANES // 2

    def get(d):
        block = read(d)
        back = pltpu.roll(block, half, 1)
        return (
            block,
            back,
            jnp.broadcast_to(block[:, members : members + 1], block.shape),
            jnp.broadcast_to(back[:, members : members + 1], block.shape),
        )

    return get


def tables_of(rates, axis, reverse):
    width = rates.shape[axis]
    at = lax.broadcasted_iota(jnp.int32, rates.shape, axis)
    table = jnp.where(at == (width - 1 if reverse else 0), 0.0, rates)
    tables, step = [], 1
    while step < width:
        tables.append(table)
        table = table * pltpu.roll(table, width - step if reverse else step, axis)
        step *= 2
    return tables


def sweep(values, tables, axis, reverse):
    width = values.shape[axis]
    step = 1
    for table in tables:
        values = values + table * pltpu.roll(values, width - step if reverse else step, axis)
        step *= 2
    return values


def responses(rates, scales, axis, forward, reverse):
    at = lax.broadcasted_iota(jnp.int32, rates.shape, axis)
    product = sweep(jnp.where(at == 0, rates, 0.0), forward, axis, False)
    answer = sweep(scales * product, reverse, axis, True)
    behind = sweep(jnp.where(at == rates.shape[axis] - 1, rates, 0.0), reverse, axis, True)
    return product, answer, behind


def x_sweeps(get, count, rates, scales, take):
    forward, reverse = tables_of(rates, 0, False), tables_of(rates, 0, True)
    for k in range(count):
        ahead = sweep(get(k), forward, 0, False)
        take(k, ahead, sweep(scales * ahead, reverse, 0, True))


def send_y(get, count, response_ref, message_ref):
    last, first = response_ref[3], response_ref[4]
    rows, columns = last.shape
    lane = lax.broadcasted_iota(jnp.int32, (rows, LANES), 1)
    half = LANES // 2
    product, answer = response_ref[0][:, columns - 1 :], response_ref[1][:, :1]
    message = jnp.where(lane == count, product, jnp.where(lane == half + count, answer, 0.0))
    for k in range(count):
        weights = get(k)
        message = jnp.where(lane == k, jnp.sum(last * weights, axis=1, keepdims=True), message)
        message = jnp.where(lane == half + k, jnp.sum(first * weights, axis=1, keepdims=True), message)
    message_ref[...] = message


def split_dot(a, b, dims):
    rows = a.shape[0]
    high = a.astype(jnp.bfloat16)
    rest = a - high.astype(jnp.float32)
    middle = rest.astype(jnp.bfloat16)
    low = (rest - middle.astype(jnp.float32)).astype(jnp.bfloat16)
    parts = jnp.concatenate([high, middle, low], axis=0)
    out = lax.dot_general(parts, b, (dims, ((), ())), preferred_element_type=jnp.float32)
    return out[:rows] + (out[rows : 2 * rows] + out[2 * rows :])


def first_kernel(members, far_controls_ref, far_rates_ref, local_ref, message_ref, controls_ref, rates_ref, semaphores):
    fetches = (
        pltpu.make_async_copy(far_rates_ref, rates_ref, semaphores.at[0]),
        pltpu.make_async_copy(far_controls_ref, controls_ref, semaphores.at[1]),
    )
    for fetch in fetches:
        fetch.start()
    for fetch in fetches:
        fetch.wait()
    rates = rates_ref[...]
    rows, columns = rates.shape
    scales = jnp.sqrt(1.0 - rates * rates)
    half = row_count(members)
    forward, reverse = tables_of(rates, 0, False), tables_of(rates, 0, True)
    product, answer, behind = responses(rates, scales, 0, forward, reverse)
    local_ref[members] = answer
    local_ref[members + 1] = behind
    factor = scales / rates
    ahead, behind = factor * answer, factor * behind
    message_ref[members:half] = jnp.zeros((half - members, columns), jnp.float32)
    message_ref[half + members :] = jnp.zeros((half - members, columns), jnp.float32)
    message_ref[members : members + 1] = product[rows - 1 :]
    message_ref[members + 1 : members + 2] = jnp.sum(ahead * ahead, axis=0, keepdims=True)
    message_ref[members + 2 : members + 3] = jnp.sum(2.0 * ahead * behind, axis=0, keepdims=True)
    message_ref[members + 3 : members + 4] = jnp.sum(behind * behind, axis=0, keepdims=True)
    message_ref[half + members : half + members + 1] = answer[:1]

    def take(k, ahead, back):
        local_ref[k] = back
        message_ref[k : k + 1] = ahead[rows - 1 :]
        message_ref[half + k : half + k + 1] = back[:1]

    x_sweeps(lambda k: scales * controls_ref[k], members, rates, scales, take)


def tables_kernel(
    rates_ref,
    cells_ref,
    codes_ref,
    values_ref,
    precisions_ref,
    old_ref,
    forward_ref,
    reverse_ref,
    response_ref,
    columns_ref,
    weights_ref,
    old_sum_ref,
):
    rates = rates_ref[...]
    rows, columns = rates.shape
    scales = jnp.sqrt(1.0 - rates * rates)
    forward, reverse = tables_of(rates, 1, False), tables_of(rates, 1, True)
    for n in range(len(forward)):
        forward_ref[n] = forward[n]
        reverse_ref[n] = reverse[n]
    product, answer, behind = responses(rates, scales, 1, forward, reverse)
    lane = lax.broadcasted_iota(jnp.int32, rates.shape, 1)
    response_ref[0] = product
    response_ref[1] = answer
    response_ref[2] = behind
    response_ref[3] = jnp.where(lane == columns - 1, 1.0, pltpu.roll(behind, columns - 1, 1))
    reach = scales * jnp.where(lane == 0, 1.0, pltpu.roll(product, 1, 1))
    carried = sweep(rates * reach, reverse, 1, True)
    response_ref[4] = reach + jnp.where(lane == columns - 1, 0.0, pltpu.roll(carried, columns - 1, 1))
    cells = cells_ref[...]
    count = cells.shape[1]
    at = lax.broadcasted_iota(jnp.int32, (columns, count), 0)
    columns_ref[...] = jnp.where(at == cells % columns, 1.0, 0.0).astype(jnp.bfloat16)
    bearing = codes_ref[...].astype(jnp.float32) * (2.0 * math.pi / NDIR)
    row = lax.broadcasted_iota(jnp.int32, (rows, count), 0) == cells // columns
    weights_ref[:rows] = jnp.where(row, jnp.cos(bearing), 0.0)
    weights_ref[rows : 2 * rows] = jnp.where(row, jnp.sin(bearing), 0.0)
    weights_ref[2 * rows : 2 * rows + 1] = values_ref[...]
    weights_ref[2 * rows + 1 : 2 * rows + 2] = precisions_ref[...]
    total = jnp.zeros((rows, columns), jnp.float32)
    for k in range(old_ref.shape[0]):
        total += old_ref[k] * old_ref[k]
    old_sum_ref[...] = total


def second_kernel(members, count, *refs):
    messages = refs[:-6]
    local_ref, rates_ref, response_ref, out_ref, message_ref, states_ref = refs[-6:]
    place = lax.axis_index("gx")
    entering, backward, _ = chain(x_reader(messages, count, "gx", members), count, place)
    half = row_count(members)
    states_ref[:half] = entering
    states_ref[half:] = backward
    rates = rates_ref[...]
    scales = jnp.sqrt(1.0 - rates * rates)
    local, ahead, behind = scales, scales * local_ref[members], scales * local_ref[members + 1]

    def get(k):
        weights = (
            local * local_ref[k] + ahead * states_ref[k : k + 1] + behind * states_ref[half + k : half + k + 1]
        )
        out_ref[k] = weights
        return weights

    send_y(get, members, response_ref, message_ref)


def sweep_kernel(weights_ref, rates_ref, forward_ref, reverse_ref, out_ref):
    rates = rates_ref[...]
    scales = jnp.sqrt(1.0 - rates * rates)
    forward = [forward_ref[n] for n in range(forward_ref.shape[0])]
    reverse = [reverse_ref[n] for n in range(reverse_ref.shape[0])]
    for k in range(weights_ref.shape[0]):
        out_ref[k] = sweep(scales * sweep(weights_ref[k], forward, 1, False), reverse, 1, True)


def third_kernel(members, count, spread, *refs):
    messages = refs[:-4]
    local_ref, response_ref, anomalies_ref, out_ref = refs[-4:]
    entering, backward, _ = chain(y_reader(messages, count, "gy", members), count, lax.axis_index("gy"))
    ahead, behind = response_ref[1], response_ref[2]
    rows = ahead.shape[0]
    east, north = jnp.zeros_like(ahead), jnp.zeros_like(ahead)
    for k in range(members):
        filtered = local_ref[k] + ahead * entering[:, k : k + 1] + behind * backward[:, k : k + 1]
        east += anomalies_ref[0, k].astype(jnp.float32) * filtered
        north += anomalies_ref[1, k].astype(jnp.float32) * filtered
    out_ref[:rows] = east * spread
    out_ref[rows:] = north * spread


def fourth_kernel(members, spread, shares, *refs):
    partials = refs[:shares]
    (
        anomalies_ref,
        columns_ref,
        weights_ref,
        rates_ref,
        response_ref,
        increment_ref,
        out_ref,
        message_ref,
    ) = refs[shares:]
    rates = rates_ref[...]
    rows = rates.shape[0]
    increment = partials[0][...]
    for ref in partials[1:]:
        increment = increment + ref[...]
    increment_ref[...] = increment
    picked = split_dot(increment, columns_ref[...], ((1,), (0,)))
    weights = weights_ref[: 2 * rows]
    values, precisions = weights_ref[2 * rows : 2 * rows + 1], weights_ref[2 * rows + 1 : 2 * rows + 2]
    projected = jnp.sum(weights * picked, axis=0, keepdims=True)
    misfit = precisions * (projected - values)
    back = split_dot(weights * misfit, columns_ref[...], ((1,), (1,)))
    east = back[:rows] * rates * spread
    north = back[rows:] * rates * spread

    def get(k):
        weights = anomalies_ref[0, k].astype(jnp.float32) * east + anomalies_ref[1, k].astype(jnp.float32) * north
        out_ref[k] = weights
        return weights

    send_y(get, members, response_ref, message_ref)


def fifth_kernel(members, count, *refs):
    messages = refs[:-10]
    (
        local_ref,
        response_ref,
        y_rates_ref,
        x_rates_ref,
        x_response_ref,
        controls_ref,
        old_ref,
        old_sum_ref,
        out_ref,
        message_ref,
    ) = refs[-10:]
    entering, backward, _ = chain(y_reader(messages, count, "gy", members), count, lax.axis_index("gy"))
    y_rates, rates = y_rates_ref[...], x_rates_ref[...]
    rows, columns = rates.shape
    factor = rates * jnp.sqrt(1.0 - y_rates * y_rates) / y_rates
    ahead, behind = factor * response_ref[1], factor * response_ref[2]

    def get(k):
        return factor * local_ref[k] + ahead * entering[:, k : k + 1] + behind * backward[:, k : k + 1]

    scales = jnp.sqrt(1.0 - rates * rates)
    ratio = scales / rates
    x_ahead, x_behind = ratio * x_response_ref[members], ratio * x_response_ref[members + 1]
    sums = [jnp.zeros((rows, columns), jnp.float32)]

    def take(k, ahead, back):
        gradient = controls_ref[k] + ratio * back
        out_ref[k] = gradient
        change = gradient - old_ref[k]
        sums[0] += gradient * change
        slope = gradient + change
        message_ref[k : k + 1] = ahead[rows - 1 :]
        message_ref[members + k : members + k + 1] = back[:1]
        message_ref[2 * members + k : 2 * members + k + 1] = jnp.sum(x_ahead * slope, axis=0, keepdims=True)
        message_ref[3 * members + k : 3 * members + k + 1] = jnp.sum(x_behind * slope, axis=0, keepdims=True)

    x_sweeps(get, members, rates, scales, take)
    end = 4 * members
    message_ref[end : end + 1] = jnp.sum(sums[0], axis=0, keepdims=True)
    message_ref[end + 1 : end + 2] = jnp.sum(old_sum_ref[...], axis=0, keepdims=True)
    message_ref[end + 2 :] = jnp.zeros((message_ref.shape[0] - end - 2, columns), jnp.float32)


def sixth_kernel(members, count, *refs):
    local_ref, rates_ref, x_response_ref, gradient_ref, sums_ref, states_ref = refs[-6:]
    messages = refs[: (len(refs) - 6) // 2]
    earlier = refs[len(messages) : -6]
    read, read_earlier = source_reader(messages, count, "gx"), source_reader(earlier, count, "gx")
    half = row_count(members)
    blocks = [read(d) for d in range(count)]
    answers = [read_earlier(d) for d in range(count)]

    def get(d):
        return (
            blocks[d][:members],
            blocks[d][members : 2 * members],
            answers[d][members : members + 1],
            answers[d][half + members : half + members + 1],
        )

    entering, backward, every = chain(get, count, lax.axis_index("gx"), True)
    states_ref[:members] = entering
    states_ref[half : half + members] = backward
    rates = rates_ref[...]
    rows, columns = rates.shape
    factor = jnp.sqrt(1.0 - rates * rates) / rates
    ahead, behind = factor * x_response_ref[members], factor * x_response_ref[members + 1]
    for k in range(members):
        gradient_ref[k] = (
            local_ref[k] + ahead * states_ref[k : k + 1] + behind * states_ref[half + k : half + k + 1]
        )
    total = jnp.zeros((members, columns), jnp.float32)
    numerator, denominator = jnp.zeros((1, columns), jnp.float32), jnp.zeros((1, columns), jnp.float32)
    for d in range(count):
        block, answer = blocks[d], answers[d]
        one, two = every[d]
        squares = [answer[members + n : members + n + 1] for n in (1, 2, 3)]
        total += one * (block[2 * members : 3 * members] + squares[0] * one + squares[1] * two)
        total += two * (block[3 * members : 4 * members] + squares[2] * two)
        numerator += block[4 * members : 4 * members + 1]
        denominator += block[4 * members + 1 : 4 * members + 2]
    numerator += jnp.sum(total, axis=0, keepdims=True)
    row = lax.broadcasted_iota(jnp.int32, (SUB, columns), 0)
    sums = jnp.where(row == 0, numerator, jnp.where(row == 1, denominator, 0.0))
    packed = sums[:, :LANES]
    for at in range(LANES, columns, LANES):
        packed = packed + sums[:, at : at + LANES]
    sums_ref[...] = packed


def last_kernel(*refs):
    near_ref, old_ref, gradient_ref, far_ref, direction_ref, semaphores = refs[-6:]
    copies = [pltpu.make_async_copy(near_ref, gradient_ref, semaphores.at[0])]
    copies[0].start()
    total = refs[0][...]
    for ref in refs[1:-6]:
        total = total + ref[...]
    numerator = jnp.sum(total[:1], axis=1, keepdims=True)
    denominator = jnp.sum(total[1:2], axis=1, keepdims=True)
    ratio = numerator / denominator
    for k in range(near_ref.shape[0]):
        direction_ref[k] = ratio * old_ref[k] - near_ref[k]
    copies.append(pltpu.make_async_copy(direction_ref, far_ref, semaphores.at[1]))
    copies[1].start()
    for copy in copies:
        copy.wait()


def exchange(message, axis, count):
    if count <= 4:
        shifts = range(1, count)
        return [message] + [lax.ppermute(message, axis, [(i, (i + d) % count) for i in range(count)]) for d in shifts]
    return [lax.all_gather(message, axis)]


def shares_over(values, axis, count):
    if count == 2:
        return [values, lax.ppermute(values, axis, [(0, 1), (1, 0)])]
    return [lax.psum(values, axis)]


def shards(
    n_gx,
    n_gy,
    n_gz,
    controls,
    anomalies,
    x_rates,
    y_rates,
    obs_cells,
    obs_codes,
    obs_values,
    obs_weights,
    prev_gradient,
    prev_direction,
):
    members, rows, columns = controls.shape
    spread = 1.0 / math.sqrt(members * n_gz - 1)
    lines = 2 * row_count(members)
    observed = obs_cells.size
    depth = (columns - 1).bit_length()
    field = (members, rows, columns)
    extended = (members + 2, rows, columns)

    near = pltpu.with_memory_space_constraint
    x_response, message = call(
        functools.partial(first_kernel, members),
        (f32(*extended), f32(lines, columns)),
        [pltpu.VMEM(field, jnp.float32), pltpu.VMEM((rows, columns), jnp.float32), pltpu.SemaphoreType.DMA((2,))],
        in_specs=[HBM_SPEC, HBM_SPEC],
    )(near(controls, pltpu.HBM), near(x_rates, pltpu.HBM))
    x_messages = exchange(message, "gx", n_gx)
    forward, reverse, response, column_ones, row_weights, old_sum = call(
        tables_kernel,
        (
            f32(depth, rows, columns),
            f32(depth, rows, columns),
            f32(5, rows, columns),
            jax.ShapeDtypeStruct((columns, observed), jnp.bfloat16),
            f32(2 * rows + SUB, observed),
            f32(rows, columns),
        ),
    )(
        y_rates,
        obs_cells.reshape(1, observed),
        obs_codes.reshape(1, observed),
        obs_values.reshape(1, observed),
        obs_weights.reshape(1, observed),
        prev_gradient,
    )
    weights, message = call(
        functools.partial(second_kernel, members, n_gx),
        (f32(*field), f32(rows, LANES)),
        [pltpu.VMEM((lines, columns), jnp.float32)],
    )(*x_messages, x_response, y_rates, response)
    messages = exchange(message, "gy", n_gy)
    filtered = call(sweep_kernel, f32(*field))(weights, y_rates, forward, reverse)
    partial = call(functools.partial(third_kernel, members, n_gy, spread), f32(2 * rows, columns))(
        *messages, filtered, response, anomalies
    )
    partials = shares_over(partial, "gz", n_gz)
    increment, weights, message = call(
        functools.partial(fourth_kernel, members, spread, len(partials)),
        (f32(2 * rows, columns), f32(*field), f32(rows, LANES)),
    )(*partials, anomalies, column_ones, row_weights, y_rates, response)
    messages = exchange(message, "gy", n_gy)
    pulled = call(sweep_kernel, f32(*field))(weights, y_rates, forward, reverse)
    gradient, message = call(
        functools.partial(fifth_kernel, members, n_gy),
        (f32(*field), f32(-(-(4 * members + 2) // SUB) * SUB, columns)),
    )(*messages, pulled, response, y_rates, x_rates, x_response, controls, prev_gradient, old_sum)
    gradient, sums = call(
        functools.partial(sixth_kernel, members, n_gx),
        (f32(*field), f32(SUB, LANES)),
        [pltpu.VMEM((lines, columns), jnp.float32)],
    )(*exchange(message, "gx", n_gx), *x_messages, gradient, x_rates, x_response)
    sums = sum(shares_over(sums, "gz", n_gz))
    gradient, direction = call(
        last_kernel,
        (f32(*field), f32(*field)),
        [pltpu.VMEM(field, jnp.float32), pltpu.SemaphoreType.DMA((2,))],
        out_specs=(HBM_SPEC, HBM_SPEC),
    )(*shares_over(sums, "gy", n_gy), gradient, prev_direction)
    return gradient, direction, increment.reshape(2, rows, columns)


def solution(mesh):
    in_specs = (
        P("gz", ("grp", "gx"), "gy"),
        P(None, "gz", ("grp", "gx"), "gy"),
        P(("grp", "gx"), "gy"),
        P(("grp", "gx"), "gy"),
        P(("grp", "gx"), "gy", None),
        P(("grp", "gx"), "gy", None),
        P(("grp", "gx"), "gy", None),
        P(("grp", "gx"), "gy", None),
        P("gz", ("grp", "gx"), "gy"),
        P("gz", ("grp", "gx"), "gy"),
    )
    out_specs = (
        P("gz", ("grp", "gx"), "gy"),
        P("gz", ("grp", "gx"), "gy"),
        P(None, ("grp", "gx"), "gy"),
    )
    body = functools.partial(shards, mesh.shape["gx"], mesh.shape["gy"], mesh.shape["gz"])
    return jax.shard_map(body, mesh=mesh, in_specs=in_specs, out_specs=out_specs, check_vma=False)
```

time: 45 us -> 38.8 us (0.86)
  blocking collectives: 10.6 us -> 0 us
  waiting for transfers between devices: 13.4 us -> 16.6 us
  local copies, waits for them, and re-layouts: 1.64 us -> 0.04 us
  starting transfers between devices: 12.5 us -> 14 us
  Pallas kernels: 6.05 us -> 7.27 us
    all_to_all x1 -> x0, blocking collectives: 10.6 us -> none  [shards(): sums = lax.all_to_all(sums, ('gx', 'gy', 'gz'), 0, 0)]
    ppermute x1 -> x3, waiting for transfers between devices: 1.17 us -> 4.44 us  [shares_over(): return [values, lax.ppermute(values, axis, [(0, 1), (1, 0)])]]
    pallas_call x2 -> x4, Pallas kernels: 0.46 us -> 2.69 us  [the longest x1 1.03 us: shards(): call(sweep_kernel, f32(*field))(weights, y_rates, forward, reverse)]
    unnamed x22 -> x20, local copies, waits for them, and re-layouts: 1.64 us -> 0.04 us
    ppermute x1 -> x3, starting transfers between devices: 0.07 us -> 1.63 us  [shares_over(): return [values, lax.ppermute(values, axis, [(0, 1), (1, 0)])]]
    pallas_call x1, Pallas kernels: 1.16 us -> 0.18 us  [shards(): call(functools.partial(second_kernel, members, n_gx), (f32(*field), f32(r...]
    pallas_call x1, Pallas kernels: 1.92 us -> 0.96 us  [shards(): call(functools.partial(fourth_kernel, members, spread, len(partials)), (f...]
    pallas_call x1, Pallas kernels: 0.4 us -> 1.2 us  [shards(): call(functools.partial(first_kernel, members), (f32(*extended), f32(lines...]
  transfers between devices with their start and end apart: 9 -> 11, of which waited for: 7 -> 9; matrix products, arithmetic and copies ran while one was open for 0% -> 0% of each run, Pallas kernels for 2% -> 8%
where the time goes in v3:
time: 38.8 us; the launch traced here: 38.7 us
  waiting for transfers between devices  16.6 us (43%)
  starting transfers between devices  14 us (36%)
  Pallas kernels  7.27 us (19%)
  between operations  0.77 us (2%)
    ppermute x8, starting transfers between devices, exchange(): lax.ppermute(message, axis, [(i, (i + d) % count) for i in range(count)])  12.4 us
    ppermute x8, waiting for transfers between devices, exchange(): lax.ppermute(message, axis, [(i, (i + d) % count) for i in range(count)])  12.1 us
    ppermute x3, waiting for transfers between devices, shares_over(): return [values, lax.ppermute(values, axis, [(0, 1), (1, 0)])]  4.44 us
    ppermute x3, starting transfers between devices, shares_over(): return [values, lax.ppermute(values, axis, [(0, 1), (1, 0)])]  1.63 us
    pallas_call x1, Pallas kernels, shards(): call(functools.partial(first_kernel, members), (f32(*extended), f32(lines...  1.2 us
    pallas_call x1, Pallas kernels, shards(): call(tables_kernel, (f32(depth, rows, columns), f32(depth, rows, columns)...  1.18 us
    pallas_call x1, Pallas kernels, shards(): call(sweep_kernel, f32(*field))(weights, y_rates, forward, reverse)  1.03 us
    pallas_call x1, Pallas kernels, shards(): pulled = call(sweep_kernel, f32(*field))(weights, y_rates, forward, reverse)  1.03 us
  transfers between devices with their start and end apart: 11, of which 9 were waited for; matrix products, arithmetic and copies ran while one was open for 0% of the time, Pallas kernels for 8%

profile of v3, /device:TPU:0, one launch (start us, length us, event | category | flops | bytes accessed | tf_op | source)
XLA Modules:
  0.0 38.7 jit_solution(14366070911212520436)
XLA Ops:
  0.6 0.0 copy-start.2
  0.6 0.0 copy-start.6
  0.7 0.0 copy-start.7
  0.7 0.0 copy-start.8
  0.7 0.0 copy-start.9
  0.7 1.2 %shard_map.121 = (f32[22,8,256]{2,1,0:T(8,128)S(1)}, f32[48,256]{1,0:T(8,128)S(1)}) custom-call(f32[20,8,256]{2,1,0:T(8,128)} %refs_7_.1, f32[8,256]{1,0:T(8,128)} %refs_9_.1), custom_call_target="tpu_custom_call" | custom-call | flops 100000 | bytes 100000 | tf_op jit(solution)/shard_map/pallas_call | solution.py:489
  1.9 0.0 copy-start.3
  1.9 5.1 %collective-permute-start.2 = (f32[48,256]{1,0:T(8,128)S(1)}, f32[48,256]{1,0:T(8,128)S(1)}, u32[]{:S(2)}, u32[]{:S(2)}) collective-permute-start(f32[48,256]{1,0:T(8,128)S(1)} %get-tuple-element.22.refs_0_.refs_4_), channel_id=1, source_target_pairs={{0,12},{4,0},{8,4},{12,8},{1,13},{5,1},{9,5},{13,9},{2,14},{6,2},{... | collective-permute-start | bytes 147464 | tf_op jit(solution)/shard_map/ppermute | solution.py:455
  7.0 0.0 collective-permute-start.1
  7.0 1.0 %collective-permute-start = (f32[48,256]{1,0:T(8,128)S(1)}, f32[48,256]{1,0:T(8,128)S(1)}, u32[]{:S(2)}, u32[]{:S(2)}) collective-permute-start(f32[48,256]{1,0:T(8,128)S(1)} %get-tuple-element.22.refs_0_.refs_4_), channel_id=1, source_target_pairs={{0,4},{4,8},{8,12},{12,0},{1,5},{5,9},{9,13},{13,1},{2,6},{6,10},{... | collective-permute-start | bytes 147464 | tf_op jit(solution)/shard_map/ppermute | solution.py:455
  8.1 0.0 copy-done.2
  8.1 0.0 copy-done.6
  8.1 0.0 copy-done.7
  8.1 0.0 copy-done.8
  8.1 0.0 copy-done.9
  8.1 0.0 copy-done.3
  8.1 1.2 %shard_map.122 = (f32[8,8,256]{2,1,0:T(8,128)S(1)}, f32[8,8,256]{2,1,0:T(8,128)S(1)}, f32[5,8,256]{2,1,0:T(8,128)S(1)}, bf16[256,512]{1,0:T(8,128)(2,1)S(1)}, f3...) custom-call(f32[8,256]{1,0:T(8,128)S(1)} %copy-done.3, s32[1,512]{1,0:T(1,128)S(1)} %bitcast.5, s32[1,512]{1,0:T(1,128)S(1)} %bitcast.6, ...), custom_call_target="tpu_custom_call" | custom-call | flops 100000 | bytes 100000 | tf_op jit(solution)/shard_map/pallas_call | solution.py:496
  9.3 0.0 collective-permute-done.2.refs_3_.refs_7_
  9.3 2.8 %collective-permute-done.1.refs_2_.refs_6_ = f32[48,256]{1,0:T(8,128)S(1)} collective-permute-done((f32[48,256]{1,0:T(8,128)S(1)}, f32[48,256]{1,0:T(8,128)S(1)}, u32[]{:S(2)}, u32[]{:S(2)}) %collective-permute-start.1) | collective-permute-done | bytes 49184 | tf_op jit(solution)/shard_map/ppermute | solution.py:455
  12.0 0.9 %collective-permute-done.refs_1_.refs_5_ = f32[48,256]{1,0:T(8,128)S(1)} collective-permute-done((f32[48,256]{1,0:T(8,128)S(1)}, f32[48,256]{1,0:T(8,128)S(1)}, u32[]{:S(2)}, u32[]{:S(2)}) %collective-permute-start) | collective-permute-done | bytes 49184 | tf_op jit(solution)/shard_map/ppermute | solution.py:455
  12.9 0.2 shard_map.123
  13.1 1.6 %collective-permute-start.3 = (f32[8,128]{1,0:T(8,128)S(1)}, f32[8,128]{1,0:T(8,128)S(1)}, u32[]{:S(2)}, u32[]{:S(2)}) collective-permute-start(f32[8,128]{1,0:T(8,128)S(1)} %get-tuple-element.25.refs_0_), channel_id=1, source_target_pairs={{0,2},{2,0},{1,3},{3,1},{4,6},{6,4},{5,7},{7,5},{8,10},{10,8},{9,1... | collective-permute-start | bytes 12296 | tf_op jit(solution)/shard_map/ppermute | solution.py:455
  14.7 0.0 copy-start
  14.7 1.0 %shard_map.124.refs_2_ = f32[20,8,256]{2,1,0:T(8,128)S(1)} custom-call(f32[20,8,256]{2,1,0:T(8,128)S(1)} %get-tuple-element.26.weights_ref, f32[8,256]{1,0:T(8,128)S(1)} %copy-done.3, f32[8,8,256]{2,1,0:T(8,128)S(1)} %get-tuple-element.27.forward_ref, f32[8,8,256]{2,1,0:T(8,128)S(1)} %get-tuple-element.28.reverse_ref), custom_call_target="tpu_custom_call" | custom-call | flops 100000 | bytes 100000 | tf_op jit(solution)/shard_map/pallas_call | solution.py:520
  15.7 1.1 %collective-permute-done.3.refs_1_ = f32[8,128]{1,0:T(8,128)S(1)} collective-permute-done((f32[8,128]{1,0:T(8,128)S(1)}, f32[8,128]{1,0:T(8,128)S(1)}, u32[]{:S(2)}, u32[]{:S(2)}) %collective-permute-start.3) | collective-permute-done | bytes 4128 | tf_op jit(solution)/shard_map/ppermute | solution.py:455
  16.8 0.0 copy-done
  16.8 0.3 shard_map.125.refs_0_
  17.0 0.1 collective-permute-start.4
  17.1 1.2 %collective-permute-done.4.refs_1_ = f32[16,256]{1,0:T(8,128)S(1)} collective-permute-done((f32[16,256]{1,0:T(8,128)S(1)}, f32[16,256]{1,0:T(8,128)S(1)}, u32[]{:S(2)}, u32[]{:S(2)}) %collective-permute-start.4) | collective-permute-done | bytes 16416 | tf_op jit(solution)/shard_map/ppermute | solution.py:461
  18.3 1.0 %shard_map.126 = (f32[16,256]{1,0:T(8,128)}, f32[20,8,256]{2,1,0:T(8,128)S(1)}, f32[8,128]{1,0:T(8,128)S(1)}) custom-call(f32[16,256]{1,0:T(8,128)S(1)} %shard_map.125.refs_0_, f32[16,256]{1,0:T(8,128)S(1)} %collective-permute-done.4.refs_1_, bf16[2,20,8,256]{3,2,1,0:T(8,128)(2,1)S(1)} %copy-done, bf16[256,512]{1,0:T(8,128)(2,1)S(1)} %get-tuple-element.29.refs_3_, ...), custom_call_target="tpu_custom_call" | custom-call | flops 100000 | bytes 100000 | tf_op jit(solution)/shard_map/pallas_call | solution.py:525
  19.2 1.5 %collective-permute-start.5 = (f32[8,128]{1,0:T(8,128)S(1)}, f32[8,128]{1,0:T(8,128)S(1)}, u32[]{:S(2)}, u32[]{:S(2)}) collective-permute-start(f32[8,128]{1,0:T(8,128)S(1)} %get-tuple-element.31.refs_0_), channel_id=1, source_target_pairs={{0,2},{2,0},{1,3},{3,1},{4,6},{6,4},{5,7},{7,5},{8,10},{10,8},{9,1... | collective-permute-start | bytes 12296 | tf_op jit(solution)/shard_map/ppermute | solution.py:455
  20.7 0.0 copy-start.1
  20.7 0.0 copy-start.5
  20.7 1.0 %shard_map.127.refs_2_ = f32[20,8,256]{2,1,0:T(8,128)S(1)} custom-call(f32[20,8,256]{2,1,0:T(8,128)S(1)} %get-tuple-element.32.weights_ref, f32[8,256]{1,0:T(8,128)S(1)} %copy-done.3, f32[8,8,256]{2,1,0:T(8,128)S(1)} %get-tuple-element.27.forward_ref, f32[8,8,256]{2,1,0:T(8,128)S(1)} %get-tuple-element.28.reverse_ref), custom_call_target="tpu_custom_call" | custom-call | flops 100000 | bytes 100000 | tf_op jit(solution)/shard_map/pallas_call | solution.py:530
  21.8 1.1 %collective-permute-done.5.refs_1_ = f32[8,128]{1,0:T(8,128)S(1)} collective-permute-done((f32[8,128]{1,0:T(8,128)S(1)}, f32[8,128]{1,0:T(8,128)S(1)}, u32[]{:S(2)}, u32[]{:S(2)}) %collective-permute-start.5) | collective-permute-done | bytes 4128 | tf_op jit(solution)/shard_map/ppermute | solution.py:455
  22.9 0.0 copy-done.1
  22.9 0.0 copy-done.5
  22.9 0.5 %shard_map.128 = (f32[20,8,256]{2,1,0:T(8,128)S(1)}, f32[88,256]{1,0:T(8,128)S(1)}) custom-call(f32[8,128]{1,0:T(8,128)S(1)} %get-tuple-element.31.refs_0_, f32[8,128]{1,0:T(8,128)S(1)} %collective-permute-done.5.refs_1_, f32[20,8,256]{2,1,0:T(8,128)S(1)} %shard_map.127.refs_2_, f32[5,8,256]{2,1,0:T(8,128)S(1)} %get-tuple-element.24.refs_6_.refs_3_, ...), custom_call_target="tpu_custom_call" | custom-call | flops 100000 | bytes 100000 | tf_op jit(solution)/shard_map/pallas_call | solution.py:531
  23.3 1.3 %collective-permute-start.8 = (f32[88,256]{1,0:T(8,128)S(1)}, f32[88,256]{1,0:T(8,128)S(1)}, u32[]{:S(2)}, u32[]{:S(2)}) collective-permute-start(f32[88,256]{1,0:T(8,128)S(1)} %get-tuple-element.34.refs_0_), channel_id=1, source_target_pairs={{0,12},{4,0},{8,4},{12,8},{1,13},{5,1},{9,5},{13,9},{2,14},{6,2},{... | collective-permute-start | bytes 270344 | tf_op jit(solution)/shard_map/ppermute | solution.py:455
  24.6 0.0 collective-permute-start.7
  24.6 1.9 %collective-permute-start.6 = (f32[88,256]{1,0:T(8,128)S(1)}, f32[88,256]{1,0:T(8,128)S(1)}, u32[]{:S(2)}, u32[]{:S(2)}) collective-permute-start(f32[88,256]{1,0:T(8,128)S(1)} %get-tuple-element.34.refs_0_), channel_id=1, source_target_pairs={{0,4},{4,8},{8,12},{12,0},{1,5},{5,9},{9,13},{13,1},{2,6},{6,10},{... | collective-permute-start | bytes 270344 | tf_op jit(solution)/shard_map/ppermute | solution.py:455
  26.5 1.8 %collective-permute-done.8.refs_3_ = f32[88,256]{1,0:T(8,128)S(1)} collective-permute-done((f32[88,256]{1,0:T(8,128)S(1)}, f32[88,256]{1,0:T(8,128)S(1)}, u32[]{:S(2)}, u32[]{:S(2)}) %collective-permute-start.8) | collective-permute-done | bytes 90144 | tf_op jit(solution)/shard_map/ppermute | solution.py:455
  28.3 4.6 %collective-permute-done.7.refs_2_ = f32[88,256]{1,0:T(8,128)S(1)} collective-permute-done((f32[88,256]{1,0:T(8,128)S(1)}, f32[88,256]{1,0:T(8,128)S(1)}, u32[]{:S(2)}, u32[]{:S(2)}) %collective-permute-start.7) | collective-permute-done | bytes 90144 | tf_op jit(solution)/shard_map/ppermute | solution.py:455
  32.9 0.0 collective-permute-done.6.refs_1_
  32.9 0.0 copy-start.4
  32.9 0.2 shard_map.129
  33.0 0.1 collective-permute-start.9
  33.1 1.2 %collective-permute-done.9 = f32[8,128]{1,0:T(8,128)S(1)} collective-permute-done((f32[8,128]{1,0:T(8,128)S(1)}, f32[8,128]{1,0:T(8,128)S(1)}, u32[]{:S(2)}, u32[]{:S(2)}) %collective-permute-start.9) | collective-permute-done | bytes 4128 | tf_op jit(solution)/shard_map/ppermute | solution.py:461
  34.2 1.5 %collective-permute-start.10 = (f32[8,128]{1,0:T(8,128)S(1)}, f32[8,128]{1,0:T(8,128)S(1)}, u32[]{:S(2)}, u32[]{:S(2)}) collective-permute-start(f32[8,128]{1,0:T(8,128)S(1)} %add.3.refs_0_), channel_id=1, source_target_pairs={{0,2},{2,0},{1,3},{3,1},{4,6},{6,4},{5,7},{7,5},{8,10},{10,8},{9,1... | collective-permute-start | bytes 12296 | tf_op jit(solution)/shard_map/ppermute | solution.py:461
  35.7 2.1 %collective-permute-done.10.refs_1_ = f32[8,128]{1,0:T(8,128)S(1)} collective-permute-done((f32[8,128]{1,0:T(8,128)S(1)}, f32[8,128]{1,0:T(8,128)S(1)}, u32[]{:S(2)}, u32[]{:S(2)}) %collective-permute-start.10) | collective-permute-done | bytes 4128 | tf_op jit(solution)/shard_map/ppermute | solution.py:461
  37.9 0.0 copy-done.4
  37.9 0.8 %shard_map.130 = (f32[20,8,256]{2,1,0:T(8,128)}, f32[20,8,256]{2,1,0:T(8,128)}) custom-call(f32[8,128]{1,0:T(8,128)S(1)} %add.3.refs_0_, f32[8,128]{1,0:T(8,128)S(1)} %collective-permute-done.10.refs_1_, f32[20,8,256]{2,1,0:T(8,128)S(1)} %get-tuple-element.37.refs_2_, f32[20,8,256]{2,1,0:T(8,128)S(1)} %copy-done.4), custom_call_target="tpu_custom_call" | custom-call | flops 100000 | bytes 100000 | tf_op jit(solution)/shard_map/pallas_call | solution.py:541
  (1 shorter events, 0.0 us)
Async XLA Ops:
  0.6 7.4 %copy-start.2 = (f32[20,8,256]{2,1,0:T(8,128)S(1)}, f32[20,8,256]{2,1,0:T(8,128)}, u32[]{:S(2)}) copy-start(f32[20,8,256]{2,1,0:T(8,128)} %refs_8_.1) | copy-start | bytes 491524
  0.6 7.4 %copy-start.6 = (s32[1,1,512]{2,1,0:T(1,128)S(1)}, s32[1,1,512]{2,1,0:T(1,128)}, u32[]{:S(2)}) copy-start(s32[1,1,512]{2,1,0:T(1,128)} %param.14) | copy-start | bytes 6148
  0.7 7.4 %copy-start.7 = (s32[1,1,512]{2,1,0:T(1,128)S(1)}, s32[1,1,512]{2,1,0:T(1,128)}, u32[]{:S(2)}) copy-start(s32[1,1,512]{2,1,0:T(1,128)} %param.15) | copy-start | bytes 6148
  0.7 7.4 %copy-start.8 = (f32[1,1,512]{2,1,0:T(1,128)S(1)}, f32[1,1,512]{2,1,0:T(1,128)}, u32[]{:S(2)}) copy-start(f32[1,1,512]{2,1,0:T(1,128)} %param.16) | copy-start | bytes 6148
  0.7 7.4 %copy-start.9 = (f32[1,1,512]{2,1,0:T(1,128)S(1)}, f32[1,1,512]{2,1,0:T(1,128)}, u32[]{:S(2)}) copy-start(f32[1,1,512]{2,1,0:T(1,128)} %param.17) | copy-start | bytes 6148
  1.9 6.2 %copy-start.3 = (f32[8,256]{1,0:T(8,128)S(1)}, f32[8,256]{1,0:T(8,128)}, u32[]{:S(2)}) copy-start(f32[8,256]{1,0:T(8,128)} %refs_4_.3) | copy-start | bytes 24580
  1.9 7.4 %collective-permute-start.2 = (f32[48,256]{1,0:T(8,128)S(1)}, f32[48,256]{1,0:T(8,128)S(1)}, u32[]{:S(2)}, u32[]{:S(2)}) collective-permute-start(f32[48,256]{1,0:T(8,128)S(1)} %get-tuple-element.22.refs_0_.refs_4_), channel_id=1, source_target_pairs={{0,12},{4,0},{8,4},{12,8},{1,13},{5,1},{9,5},{13,9},{2,14},{6,2},{... | collective-permute-start | bytes 147464 | tf_op jit(solution)/shard_map/ppermute | solution.py:455
  7.0 5.0 %collective-permute-start.1 = (f32[48,256]{1,0:T(8,128)S(1)}, f32[48,256]{1,0:T(8,128)S(1)}, u32[]{:S(2)}, u32[]{:S(2)}) collective-permute-start(f32[48,256]{1,0:T(8,128)S(1)} %get-tuple-element.22.refs_0_.refs_4_), channel_id=1, source_target_pairs={{0,8},{4,12},{8,0},{12,4},{1,9},{5,13},{9,1},{13,5},{2,10},{6,14},... | collective-permute-start | bytes 147464 | tf_op jit(solution)/shard_map/ppermute | solution.py:455
  7.0 5.9 %collective-permute-start = (f32[48,256]{1,0:T(8,128)S(1)}, f32[48,256]{1,0:T(8,128)S(1)}, u32[]{:S(2)}, u32[]{:S(2)}) collective-permute-start(f32[48,256]{1,0:T(8,128)S(1)} %get-tuple-element.22.refs_0_.refs_4_), channel_id=1, source_target_pairs={{0,4},{4,8},{8,12},{12,0},{1,5},{5,9},{9,13},{13,1},{2,6},{6,10},{... | collective-permute-start | bytes 147464 | tf_op jit(solution)/shard_map/ppermute | solution.py:455
  13.1 3.7 %collective-permute-start.3 = (f32[8,128]{1,0:T(8,128)S(1)}, f32[8,128]{1,0:T(8,128)S(1)}, u32[]{:S(2)}, u32[]{:S(2)}) collective-permute-start(f32[8,128]{1,0:T(8,128)S(1)} %get-tuple-element.25.refs_0_), channel_id=1, source_target_pairs={{0,2},{2,0},{1,3},{3,1},{4,6},{6,4},{5,7},{7,5},{8,10},{10,8},{9,1... | collective-permute-start | bytes 12296 | tf_op jit(solution)/shard_map/ppermute | solution.py:455
  14.7 2.1 %copy-start = (bf16[2,20,8,256]{3,2,1,0:T(8,128)(2,1)S(1)}, bf16[2,20,8,256]{3,2,1,0:T(8,128)(2,1)}, u32[]{:S(2)}) copy-start(bf16[2,20,8,256]{3,2,1,0:T(8,128)(2,1)} %refs_2_.1) | copy-start | bytes 491524
  17.0 1.2 %collective-permute-start.4 = (f32[16,256]{1,0:T(8,128)S(1)}, f32[16,256]{1,0:T(8,128)S(1)}, u32[]{:S(2)}, u32[]{:S(2)}) collective-permute-start(f32[16,256]{1,0:T(8,128)S(1)} %shard_map.125.refs_0_), channel_id=1, source_target_pairs={{0,1},{1,0},{2,3},{3,2},{4,5},{5,4},{6,7},{7,6},{8,9},{9,8},{10,11... | collective-permute-start | bytes 49160 | tf_op jit(solution)/shard_map/ppermute | solution.py:461
  19.2 3.6 %collective-permute-start.5 = (f32[8,128]{1,0:T(8,128)S(1)}, f32[8,128]{1,0:T(8,128)S(1)}, u32[]{:S(2)}, u32[]{:S(2)}) collective-permute-start(f32[8,128]{1,0:T(8,128)S(1)} %get-tuple-element.31.refs_0_), channel_id=1, source_target_pairs={{0,2},{2,0},{1,3},{3,1},{4,6},{6,4},{5,7},{7,5},{8,10},{10,8},{9,1... | collective-permute-start | bytes 12296 | tf_op jit(solution)/shard_map/ppermute | solution.py:455
  20.7 2.1 %copy-start.1 = (f32[20,8,256]{2,1,0:T(8,128)S(1)}, f32[20,8,256]{2,1,0:T(8,128)}, u32[]{:S(2)}) copy-start(f32[20,8,256]{2,1,0:T(8,128)} %refs_7_.1) | copy-start | bytes 491524
  20.7 2.1 %copy-start.5 = (f32[8,256]{1,0:T(8,128)S(1)}, f32[8,256]{1,0:T(8,128)}, u32[]{:S(2)}) copy-start(f32[8,256]{1,0:T(8,128)} %refs_9_.1) | copy-start | bytes 24580
  23.3 5.0 %collective-permute-start.8 = (f32[88,256]{1,0:T(8,128)S(1)}, f32[88,256]{1,0:T(8,128)S(1)}, u32[]{:S(2)}, u32[]{:S(2)}) collective-permute-start(f32[88,256]{1,0:T(8,128)S(1)} %get-tuple-element.34.refs_0_), channel_id=1, source_target_pairs={{0,12},{4,0},{8,4},{12,8},{1,13},{5,1},{9,5},{13,9},{2,14},{6,2},{... | collective-permute-start | bytes 270344 | tf_op jit(solution)/shard_map/ppermute | solution.py:455
  24.6 8.2 %collective-permute-start.7 = (f32[88,256]{1,0:T(8,128)S(1)}, f32[88,256]{1,0:T(8,128)S(1)}, u32[]{:S(2)}, u32[]{:S(2)}) collective-permute-start(f32[88,256]{1,0:T(8,128)S(1)} %get-tuple-element.34.refs_0_), channel_id=1, source_target_pairs={{0,8},{4,12},{8,0},{12,4},{1,9},{5,13},{9,1},{13,5},{2,10},{6,14},... | collective-permute-start | bytes 270344 | tf_op jit(solution)/shard_map/ppermute | solution.py:455
  24.6 8.2 %collective-permute-start.6 = (f32[88,256]{1,0:T(8,128)S(1)}, f32[88,256]{1,0:T(8,128)S(1)}, u32[]{:S(2)}, u32[]{:S(2)}) collective-permute-start(f32[88,256]{1,0:T(8,128)S(1)} %get-tuple-element.34.refs_0_), channel_id=1, source_target_pairs={{0,4},{4,8},{8,12},{12,0},{1,5},{5,9},{9,13},{13,1},{2,6},{6,10},{... | collective-permute-start | bytes 270344 | tf_op jit(solution)/shard_map/ppermute | solution.py:455
  32.9 5.0 %copy-start.4 = (f32[20,8,256]{2,1,0:T(8,128)S(1)}, f32[20,8,256]{2,1,0:T(8,128)}, u32[]{:S(2)}) copy-start(f32[20,8,256]{2,1,0:T(8,128)} %refs_3_.1) | copy-start | bytes 491524
  33.0 1.2 %collective-permute-start.9 = (f32[8,128]{1,0:T(8,128)S(1)}, f32[8,128]{1,0:T(8,128)S(1)}, u32[]{:S(2)}, u32[]{:S(2)}) collective-permute-start(f32[8,128]{1,0:T(8,128)S(1)} %get-tuple-element.36), channel_id=1, source_target_pairs={{0,1},{1,0},{2,3},{3,2},{4,5},{5,4},{6,7},{7,6},{8,9},{9,8},{10,11... | collective-permute-start | bytes 12296 | tf_op jit(solution)/shard_map/ppermute | solution.py:461
  34.2 3.6 %collective-permute-start.10 = (f32[8,128]{1,0:T(8,128)S(1)}, f32[8,128]{1,0:T(8,128)S(1)}, u32[]{:S(2)}, u32[]{:S(2)}) collective-permute-start(f32[8,128]{1,0:T(8,128)S(1)} %add.3.refs_0_), channel_id=1, source_target_pairs={{0,2},{2,0},{1,3},{3,1},{4,6},{6,4},{5,7},{7,5},{8,10},{10,8},{9,1... | collective-permute-start | bytes 12296 | tf_op jit(solution)/shard_map/ppermute | solution.py:461

commit v4 on v3

--- a/solution.py
+++ b/solution.py
@@ -12,6 +12,7 @@
 SUB = 8
 LANES = 128
 LIMIT = 8 * 2**20
+PIECES = 4
 VMEM_SPEC = pl.BlockSpec(memory_space=pltpu.VMEM)
 HBM_SPEC = pl.BlockSpec(memory_space=pltpu.HBM)
 
@@ -31,8 +32,26 @@
     return jax.ShapeDtypeStruct(shape, jnp.float32)
 
 
-def row_count(members):
-    return -(-(members + 4) // SUB) * SUB
+def first_rows(members):
+    return -(-(2 * members + 2) // 4) * 4
+
+
+def put(ref, row, height, value):
+    for n in range(value.shape[1] // LANES):
+        ref[n * height + row : n * height + row + 1] = value[:, n * LANES : (n + 1) * LANES]
+
+
+def block_of(message, start, count, height, columns):
+    return jnp.concatenate(
+        [message[n * height + start : n * height + start + count] for n in range(columns // LANES)], axis=1
+    )
+
+
+def folded(row):
+    total = row[:, :LANES]
+    for at in range(LANES, row.shape[1], LANES):
+        total = total + row[:, at : at + LANES]
+    return total
 
 
 def chain(get, count, place, everywhere=False):
@@ -86,14 +105,17 @@
     return lambda d: refs[0][lax.rem(place - d + count, count)]
 
 
-def x_reader(refs, count, axis, members):
+def x_reader(refs, count, axis, members, columns):
     read = source_reader(refs, count, axis)
-    half = row_count(members)
-
+    height = first_rows(members)
+
+    @functools.cache
     def get(d):
-        block = read(d)
-        out, back = block[:half], block[half:]
-        return out, back, out[members : members + 1], back[members : members + 1]
+        message = read(d)
+        return [
+            block_of(message, start, rows, height, columns)
+            for start, rows in ((0, members), (members, members), (2 * members, 1), (2 * members + 1, 1))
+        ]
 
     return get
 
@@ -102,6 +124,7 @@
     read = source_reader(refs, count, axis)
     half = LANES // 2
 
+    @functools.cache
     def get(d):
         block = read(d)
         back = pltpu.roll(block, half, 1)
@@ -176,38 +199,40 @@
     return out[:rows] + (out[rows : 2 * rows] + out[2 * rows :])
 
 
+def pieces(members):
+    size = -(-members // PIECES)
+    return [slice(at, min(at + size, members)) for at in range(0, members, size)]
+
+
 def first_kernel(members, far_controls_ref, far_rates_ref, local_ref, message_ref, controls_ref, rates_ref, semaphores):
-    fetches = (
-        pltpu.make_async_copy(far_rates_ref, rates_ref, semaphores.at[0]),
-        pltpu.make_async_copy(far_controls_ref, controls_ref, semaphores.at[1]),
-    )
+    fetches = [pltpu.make_async_copy(far_rates_ref, rates_ref, semaphores.at[0])]
+    for n, piece in enumerate(pieces(members)):
+        fetches.append(
+            pltpu.make_async_copy(far_controls_ref.at[piece], controls_ref.at[piece], semaphores.at[n + 1])
+        )
     for fetch in fetches:
         fetch.start()
-    for fetch in fetches:
-        fetch.wait()
+    fetches[0].wait()
     rates = rates_ref[...]
     rows, columns = rates.shape
     scales = jnp.sqrt(1.0 - rates * rates)
-    half = row_count(members)
+    height = first_rows(members)
     forward, reverse = tables_of(rates, 0, False), tables_of(rates, 0, True)
     product, answer, behind = responses(rates, scales, 0, forward, reverse)
     local_ref[members] = answer
     local_ref[members + 1] = behind
-    factor = scales / rates
-    ahead, behind = factor * answer, factor * behind
-    message_ref[members:half] = jnp.zeros((half - members, columns), jnp.float32)
-    message_ref[half + members :] = jnp.zeros((half - members, columns), jnp.float32)
-    message_ref[members : members + 1] = product[rows - 1 :]
-    message_ref[members + 1 : members + 2] = jnp.sum(ahead * ahead, axis=0, keepdims=True)
-    message_ref[members + 2 : members + 3] = jnp.sum(2.0 * ahead * behind, axis=0, keepdims=True)
-    message_ref[members + 3 : members + 4] = jnp.sum(behind * behind, axis=0, keepdims=True)
-    message_ref[half + members : half + members + 1] = answer[:1]
+    put(message_ref, 2 * members, height, product[rows - 1 :])
+    put(message_ref, 2 * members + 1, height, answer[:1])
+    for row in range(2 * members + 2, height):
+        put(message_ref, row, height, jnp.zeros((1, columns), jnp.float32))
 
     def take(k, ahead, back):
         local_ref[k] = back
-        message_ref[k : k + 1] = ahead[rows - 1 :]
-        message_ref[half + k : half + k + 1] = back[:1]
-
+        put(message_ref, k, height, ahead[rows - 1 :])
+        put(message_ref, members + k, height, back[:1])
+
+    for fetch in fetches[1:]:
+        fetch.wait()
     x_sweeps(lambda k: scales * controls_ref[k], members, rates, scales, take)
 
 
@@ -222,6 +247,7 @@
     reverse_ref,
     response_ref,
     columns_ref,
+    places_ref,
     weights_ref,
     old_sum_ref,
 ):
@@ -245,6 +271,7 @@
     count = cells.shape[1]
     at = lax.broadcasted_iota(jnp.int32, (columns, count), 0)
     columns_ref[...] = jnp.where(at == cells % columns, 1.0, 0.0).astype(jnp.bfloat16)
+    places_ref[...] = jnp.broadcast_to(cells % columns, (rows, count))
     bearing = codes_ref[...].astype(jnp.float32) * (2.0 * math.pi / NDIR)
     row = lax.broadcasted_iota(jnp.int32, (rows, count), 0) == cells // columns
     weights_ref[:rows] = jnp.where(row, jnp.cos(bearing), 0.0)
@@ -261,17 +288,17 @@
     messages = refs[:-6]
     local_ref, rates_ref, response_ref, out_ref, message_ref, states_ref = refs[-6:]
     place = lax.axis_index("gx")
-    entering, backward, _ = chain(x_reader(messages, count, "gx", members), count, place)
-    half = row_count(members)
-    states_ref[:half] = entering
-    states_ref[half:] = backward
+    columns = rates_ref.shape[1]
+    entering, backward, _ = chain(x_reader(messages, count, "gx", members, columns), count, place)
+    states_ref[0] = entering
+    states_ref[1] = backward
     rates = rates_ref[...]
     scales = jnp.sqrt(1.0 - rates * rates)
     local, ahead, behind = scales, scales * local_ref[members], scales * local_ref[members + 1]
 
     def get(k):
         weights = (
-            local * local_ref[k] + ahead * states_ref[k : k + 1] + behind * states_ref[half + k : half + k + 1]
+            local * local_ref[k] + ahead * states_ref[0, k : k + 1] + behind * states_ref[1, k : k + 1]
         )
         out_ref[k] = weights
         return weights
@@ -308,6 +335,7 @@
     (
         anomalies_ref,
         columns_ref,
+        places_ref,
         weights_ref,
         rates_ref,
         response_ref,
@@ -316,12 +344,24 @@
         message_ref,
     ) = refs[shares:]
     rates = rates_ref[...]
-    rows = rates.shape[0]
+    rows, columns = rates.shape
     increment = partials[0][...]
     for ref in partials[1:]:
         increment = increment + ref[...]
     increment_ref[...] = increment
-    picked = split_dot(increment, columns_ref[...], ((1,), (0,)))
+    places = places_ref[...]
+    lanes, tile = places % LANES, places // LANES
+    picked = []
+    for start in (0, rows):
+        value = jnp.zeros(places.shape, jnp.float32)
+        for n in range(columns // LANES):
+            block = increment[start : start + rows, n * LANES : (n + 1) * LANES]
+            found = [
+                jnp.take_along_axis(block, lanes[:, at : at + LANES], axis=1) for at in range(0, places.shape[1], LANES)
+            ]
+            value = jnp.where(tile == n, jnp.concatenate(found, axis=1), value)
+        picked.append(value)
+    picked = jnp.concatenate(picked, axis=0)
     weights = weights_ref[: 2 * rows]
     values, precisions = weights_ref[2 * rows : 2 * rows + 1], weights_ref[2 * rows + 1 : 2 * rows + 2]
     projected = jnp.sum(weights * picked, axis=0, keepdims=True)
@@ -372,16 +412,23 @@
         change = gradient - old_ref[k]
         sums[0] += gradient * change
         slope = gradient + change
-        message_ref[k : k + 1] = ahead[rows - 1 :]
-        message_ref[members + k : members + k + 1] = back[:1]
-        message_ref[2 * members + k : 2 * members + k + 1] = jnp.sum(x_ahead * slope, axis=0, keepdims=True)
-        message_ref[3 * members + k : 3 * members + k + 1] = jnp.sum(x_behind * slope, axis=0, keepdims=True)
-
+        put(message_ref, k, height, ahead[rows - 1 :])
+        put(message_ref, members + k, height, back[:1])
+        put(message_ref, 2 * members + k, height, jnp.sum(x_ahead * slope, axis=0, keepdims=True))
+        put(message_ref, 3 * members + k, height, jnp.sum(x_behind * slope, axis=0, keepdims=True))
+
+    height = 4 * members
     x_sweeps(get, members, rates, scales, take)
-    end = 4 * members
-    message_ref[end : end + 1] = jnp.sum(sums[0], axis=0, keepdims=True)
-    message_ref[end + 1 : end + 2] = jnp.sum(old_sum_ref[...], axis=0, keepdims=True)
-    message_ref[end + 2 :] = jnp.zeros((message_ref.shape[0] - end - 2, columns), jnp.float32)
+    blocks = columns // LANES
+    end = blocks * height
+    message_ref[end : end + 1] = folded(jnp.sum(sums[0], axis=0, keepdims=True))
+    message_ref[end + 1 : end + 2] = folded(jnp.sum(old_sum_ref[...], axis=0, keepdims=True))
+    squares = (x_ahead * x_ahead, 2.0 * x_ahead * x_behind, x_behind * x_behind)
+    for n, square in enumerate(squares):
+        put(message_ref, end + 2 + n * blocks, 1, jnp.sum(square, axis=0, keepdims=True))
+    last = end + 2 + len(squares) * blocks
+    if last < message_ref.shape[0]:
+        message_ref[last:] = jnp.zeros((message_ref.shape[0] - last, LANES), jnp.float32)
 
 
 def sixth_kernel(members, count, *refs):
@@ -389,62 +436,59 @@
     messages = refs[: (len(refs) - 6) // 2]
     earlier = refs[len(messages) : -6]
     read, read_earlier = source_reader(messages, count, "gx"), source_reader(earlier, count, "gx")
-    half = row_count(members)
-    blocks = [read(d) for d in range(count)]
-    answers = [read_earlier(d) for d in range(count)]
+    rows, columns = rates_ref.shape
+    height, early_height = 4 * members, first_rows(members)
+    messages, earlier = [read(d) for d in range(count)], [read_earlier(d) for d in range(count)]
+    outs = [[block_of(message, n * members, members, height, columns) for n in range(4)] for message in messages]
+    answers = [[block_of(message, 2 * members + n, 1, early_height, columns) for n in range(2)] for message in earlier]
 
     def get(d):
-        return (
-            blocks[d][:members],
-            blocks[d][members : 2 * members],
-            answers[d][members : members + 1],
-            answers[d][half + members : half + members + 1],
-        )
+        return outs[d][0], outs[d][1], answers[d][0], answers[d][1]
 
     entering, backward, every = chain(get, count, lax.axis_index("gx"), True)
-    states_ref[:members] = entering
-    states_ref[half : half + members] = backward
+    states_ref[0] = entering
+    states_ref[1] = backward
     rates = rates_ref[...]
-    rows, columns = rates.shape
     factor = jnp.sqrt(1.0 - rates * rates) / rates
     ahead, behind = factor * x_response_ref[members], factor * x_response_ref[members + 1]
     for k in range(members):
         gradient_ref[k] = (
-            local_ref[k] + ahead * states_ref[k : k + 1] + behind * states_ref[half + k : half + k + 1]
+            local_ref[k] + ahead * states_ref[0, k : k + 1] + behind * states_ref[1, k : k + 1]
         )
     total = jnp.zeros((members, columns), jnp.float32)
-    numerator, denominator = jnp.zeros((1, columns), jnp.float32), jnp.zeros((1, columns), jnp.float32)
+    sums = jnp.zeros((2, LANES), jnp.float32)
+    blocks = columns // LANES
+    end = blocks * height
     for d in range(count):
-        block, answer = blocks[d], answers[d]
+        message = messages[d]
         one, two = every[d]
-        squares = [answer[members + n : members + n + 1] for n in (1, 2, 3)]
-        total += one * (block[2 * members : 3 * members] + squares[0] * one + squares[1] * two)
-        total += two * (block[3 * members : 4 * members] + squares[2] * two)
-        numerator += block[4 * members : 4 * members + 1]
-        denominator += block[4 * members + 1 : 4 * members + 2]
-    numerator += jnp.sum(total, axis=0, keepdims=True)
-    row = lax.broadcasted_iota(jnp.int32, (SUB, columns), 0)
-    sums = jnp.where(row == 0, numerator, jnp.where(row == 1, denominator, 0.0))
-    packed = sums[:, :LANES]
-    for at in range(LANES, columns, LANES):
-        packed = packed + sums[:, at : at + LANES]
-    sums_ref[...] = packed
+        squares = [block_of(message, end + 2 + n * blocks, 1, 1, columns) for n in range(3)]
+        total += one * (outs[d][2] + squares[0] * one + squares[1] * two)
+        total += two * (outs[d][3] + squares[2] * two)
+        sums += message[end : end + 2]
+    sums_ref[...] = jnp.zeros(sums_ref.shape, jnp.float32)
+    sums_ref[:1] = sums[:1] + folded(jnp.sum(total, axis=0, keepdims=True))
+    sums_ref[1:2] = sums[1:]
 
 
 def last_kernel(*refs):
     near_ref, old_ref, gradient_ref, far_ref, direction_ref, semaphores = refs[-6:]
-    copies = [pltpu.make_async_copy(near_ref, gradient_ref, semaphores.at[0])]
-    copies[0].start()
+    members = near_ref.shape[0]
+    parts = pieces(members)
+    copies = []
+    for n, piece in enumerate(parts):
+        copies.append(pltpu.make_async_copy(near_ref.at[piece], gradient_ref.at[piece], semaphores.at[n]))
+        copies[-1].start()
     total = refs[0][...]
     for ref in refs[1:-6]:
         total = total + ref[...]
-    numerator = jnp.sum(total[:1], axis=1, keepdims=True)
-    denominator = jnp.sum(total[1:2], axis=1, keepdims=True)
-    ratio = numerator / denominator
-    for k in range(near_ref.shape[0]):
-        direction_ref[k] = ratio * old_ref[k] - near_ref[k]
-    copies.append(pltpu.make_async_copy(direction_ref, far_ref, semaphores.at[1]))
-    copies[1].start()
+    total = jnp.sum(total, axis=1, keepdims=True)
+    ratio = total[:1] / total[1:2]
+    for n, piece in enumerate(parts):
+        for k in range(piece.start, piece.stop):
+            direction_ref[k] = ratio * old_ref[k] - near_ref[k]
+        copies.append(pltpu.make_async_copy(direction_ref.at[piece], far_ref.at[piece], semaphores.at[PIECES + n]))
+        copies[-1].start()
     for copy in copies:
         copy.wait()
 
@@ -460,6 +504,12 @@
     if count == 2:
         return [values, lax.ppermute(values, axis, [(0, 1), (1, 0)])]
     return [lax.psum(values, axis)]
+
+
+def crossed_shares(values, n_gy, n_gz):
+    if n_gy == 2 and n_gz == 2:
+        return [values, lax.ppermute(values, ("gy", "gz"), [(i, 3 - i) for i in range(4)])]
+    return shares_over(values, "gy", n_gy)
 
 
 def shards(
@@ -479,7 +529,8 @@
 ):
     members, rows, columns = controls.shape
     spread = 1.0 / math.sqrt(members * n_gz - 1)
-    lines = 2 * row_count(members)
+    blocks = columns // LANES
+    lines = blocks * first_rows(members)
     observed = obs_cells.size
     depth = (columns - 1).bit_length()
     field = (members, rows, columns)
@@ -488,18 +539,19 @@
     near = pltpu.with_memory_space_constraint
     x_response, message = call(
         functools.partial(first_kernel, members),
-        (f32(*extended), f32(lines, columns)),
-        [pltpu.VMEM(field, jnp.float32), pltpu.VMEM((rows, columns), jnp.float32), pltpu.SemaphoreType.DMA((2,))],
+        (f32(*extended), f32(lines, LANES)),
+        [pltpu.VMEM(field, jnp.float32), pltpu.VMEM((rows, columns), jnp.float32), pltpu.SemaphoreType.DMA((PIECES + 1,))],
         in_specs=[HBM_SPEC, HBM_SPEC],
     )(near(controls, pltpu.HBM), near(x_rates, pltpu.HBM))
     x_messages = exchange(message, "gx", n_gx)
-    forward, reverse, response, column_ones, row_weights, old_sum = call(
+    forward, reverse, response, column_ones, places, row_weights, old_sum = call(
         tables_kernel,
         (
             f32(depth, rows, columns),
             f32(depth, rows, columns),
             f32(5, rows, columns),
             jax.ShapeDtypeStruct((columns, observed), jnp.bfloat16),
+            jax.ShapeDtypeStruct((rows, observed), jnp.int32),
             f32(2 * rows + SUB, observed),
             f32(rows, columns),
         ),
@@ -514,7 +566,7 @@
     weights, message = call(
         functools.partial(second_kernel, members, n_gx),
         (f32(*field), f32(rows, LANES)),
-        [pltpu.VMEM((lines, columns), jnp.float32)],
+        [pltpu.VMEM((2, members, columns), jnp.float32)],
     )(*x_messages, x_response, y_rates, response)
     messages = exchange(message, "gy", n_gy)
     filtered = call(sweep_kernel, f32(*field))(weights, y_rates, forward, reverse)
@@ -525,25 +577,25 @@
     increment, weights, message = call(
         functools.partial(fourth_kernel, members, spread, len(partials)),
         (f32(2 * rows, columns), f32(*field), f32(rows, LANES)),
-    )(*partials, anomalies, column_ones, row_weights, y_rates, response)
+    )(*partials, anomalies, column_ones, places, row_weights, y_rates, response)
     messages = exchange(message, "gy", n_gy)
     pulled = call(sweep_kernel, f32(*field))(weights, y_rates, forward, reverse)
     gradient, message = call(
         functools.partial(fifth_kernel, members, n_gy),
-        (f32(*field), f32(-(-(4 * members + 2) // SUB) * SUB, columns)),
+        (f32(*field), f32(-(-(blocks * (4 * members + 3) + 2) // SUB) * SUB, LANES)),
     )(*messages, pulled, response, y_rates, x_rates, x_response, controls, prev_gradient, old_sum)
     gradient, sums = call(
         functools.partial(sixth_kernel, members, n_gx),
         (f32(*field), f32(SUB, LANES)),
-        [pltpu.VMEM((lines, columns), jnp.float32)],
+        [pltpu.VMEM((2, members, columns), jnp.float32)],
     )(*exchange(message, "gx", n_gx), *x_messages, gradient, x_rates, x_response)
     sums = sum(shares_over(sums, "gz", n_gz))
     gradient, direction = call(
         last_kernel,
         (f32(*field), f32(*field)),
-        [pltpu.VMEM(field, jnp.float32), pltpu.SemaphoreType.DMA((2,))],
+        [pltpu.VMEM(field, jnp.float32), pltpu.SemaphoreType.DMA((2 * PIECES,))],
         out_specs=(HBM_SPEC, HBM_SPEC),
-    )(*shares_over(sums, "gy", n_gy), gradient, prev_direction)
+    )(*crossed_shares(sums, n_gy, n_gz), gradient, prev_direction)
     return gradient, direction, increment.reshape(2, rows, columns)
 
 

time: 38.8 us -> 37.7 us (0.972)
  waiting for transfers between devices: 16.6 us -> 15.8 us
    ppermute x3 -> x2, waiting for transfers between devices: 4.44 us -> 2.32 us  [shares_over(): return [values, lax.ppermute(values, axis, [(0, 1), (1, 0)])]]
    ppermute x0 -> x1, waiting for transfers between devices: none -> 1.77 us  [crossed_shares(): lax.ppermute(values, ('gy', 'gz'), [(i, 3 - i) for i in range(4)])]
    ppermute x3 -> x2, starting transfers between devices: 1.63 us -> 0.14 us  [shares_over(): return [values, lax.ppermute(values, axis, [(0, 1), (1, 0)])]]
    ppermute x0 -> x1, starting transfers between devices: none -> 1.26 us  [crossed_shares(): lax.ppermute(values, ('gy', 'gz'), [(i, 3 - i) for i in range(4)])]
  transfers between devices with their start and end apart: 11 -> 11, of which waited for: 9 -> 9; matrix products, arithmetic and copies ran while one was open for 0% -> 0% of each run, Pallas kernels for 8% -> 9%
where the time goes in v4:
time: 37.7 us; the launch traced here: 37.6 us
  waiting for transfers between devices  15.8 us (42%)
  starting transfers between devices  13.8 us (37%)
  Pallas kernels  7.13 us (19%)
  between operations  0.78 us (2%)
    ppermute x8, starting transfers between devices, exchange(): lax.ppermute(message, axis, [(i, (i + d) % count) for i in range(count)])  12.4 us
    ppermute x8, waiting for transfers between devices, exchange(): lax.ppermute(message, axis, [(i, (i + d) % count) for i in range(count)])  11.7 us
    ppermute x2, waiting for transfers between devices, shares_over(): return [values, lax.ppermute(values, axis, [(0, 1), (1, 0)])]  2.32 us
    ppermute x1, waiting for transfers between devices, crossed_shares(): lax.ppermute(values, ('gy', 'gz'), [(i, 3 - i) for i in range(4)])  1.77 us
    ppermute x1, starting transfers between devices, crossed_shares(): lax.ppermute(values, ('gy', 'gz'), [(i, 3 - i) for i in range(4)])  1.26 us
    pallas_call x1, Pallas kernels, shards(): call(tables_kernel, (f32(depth, rows, columns), f32(depth, rows, columns)...  1.18 us
    pallas_call x1, Pallas kernels, shards(): call(functools.partial(first_kernel, members), (f32(*extended), f32(lines...  1.1 us
    pallas_call x1, Pallas kernels, shards(): pulled = call(sweep_kernel, f32(*field))(weights, y_rates, forward, reverse)  1.03 us
  transfers between devices with their start and end apart: 11, of which 9 were waited for; matrix products, arithmetic and copies ran while one was open for 0% of the time, Pallas kernels for 9%

profile of v4, /device:TPU:0, one launch (start us, length us, event | category | flops | bytes accessed | tf_op | source)
XLA Modules:
  0.0 37.6 jit_solution(16439392698655963184)
XLA Ops:
  0.6 0.0 copy-start.2
  0.6 0.0 copy-start.6
  0.7 0.0 copy-start.7
  0.7 0.0 copy-start.8
  0.7 0.0 copy-start.9
  0.7 1.1 %shard_map.121 = (f32[22,8,256]{2,1,0:T(8,128)S(1)}, f32[88,128]{1,0:T(8,128)S(1)}) custom-call(f32[20,8,256]{2,1,0:T(8,128)} %refs_7_.1, f32[8,256]{1,0:T(8,128)} %refs_9_.1), custom_call_target="tpu_custom_call" | custom-call | flops 100000 | bytes 100000 | tf_op jit(solution)/shard_map/pallas_call | solution.py:540
  1.8 0.0 copy-start.3
  1.8 5.1 %collective-permute-start.2 = (f32[88,128]{1,0:T(8,128)S(1)}, f32[88,128]{1,0:T(8,128)S(1)}, u32[]{:S(2)}, u32[]{:S(2)}) collective-permute-start(f32[88,128]{1,0:T(8,128)S(1)} %get-tuple-element.23.refs_0_.refs_4_), channel_id=1, source_target_pairs={{0,12},{4,0},{8,4},{12,8},{1,13},{5,1},{9,5},{13,9},{2,14},{6,2},{... | collective-permute-start | bytes 135176 | tf_op jit(solution)/shard_map/ppermute | solution.py:499
  6.9 0.0 collective-permute-start.1
  6.9 1.0 %collective-permute-start = (f32[88,128]{1,0:T(8,128)S(1)}, f32[88,128]{1,0:T(8,128)S(1)}, u32[]{:S(2)}, u32[]{:S(2)}) collective-permute-start(f32[88,128]{1,0:T(8,128)S(1)} %get-tuple-element.23.refs_0_.refs_4_), channel_id=1, source_target_pairs={{0,4},{4,8},{8,12},{12,0},{1,5},{5,9},{9,13},{13,1},{2,6},{6,10},{... | collective-permute-start | bytes 135176 | tf_op jit(solution)/shard_map/ppermute | solution.py:499
  7.9 0.0 copy-done.2
  7.9 0.0 copy-done.6
  8.0 0.0 copy-done.7
  8.0 0.0 copy-done.8
  8.0 0.0 copy-done.9
  8.0 0.0 copy-done.3
  8.0 1.2 %shard_map.122 = (f32[8,8,256]{2,1,0:T(8,128)S(1)}, f32[8,8,256]{2,1,0:T(8,128)S(1)}, f32[5,8,256]{2,1,0:T(8,128)S(1)}, bf16[256,512]{1,0:T(8,128)(2,1)S(1)}, s3...) custom-call(f32[8,256]{1,0:T(8,128)S(1)} %copy-done.3, s32[1,512]{1,0:T(1,128)S(1)} %bitcast.5, ...), custom_call_target="tpu_custom_call" | custom-call | flops 100000 | bytes 100000 | tf_op jit(solution)/shard_map/pallas_call | solution.py:547
  9.2 0.0 collective-permute-done.2.refs_3_.refs_7_
  9.2 2.7 %collective-permute-done.1.refs_2_.refs_6_ = f32[88,128]{1,0:T(8,128)S(1)} collective-permute-done((f32[88,128]{1,0:T(8,128)S(1)}, f32[88,128]{1,0:T(8,128)S(1)}, u32[]{:S(2)}, u32[]{:S(2)}) %collective-permute-start.1) | collective-permute-done | bytes 45088 | tf_op jit(solution)/shard_map/ppermute | solution.py:499
  11.9 0.9 %collective-permute-done.refs_1_.refs_5_ = f32[88,128]{1,0:T(8,128)S(1)} collective-permute-done((f32[88,128]{1,0:T(8,128)S(1)}, f32[88,128]{1,0:T(8,128)S(1)}, u32[]{:S(2)}, u32[]{:S(2)}) %collective-permute-start) | collective-permute-done | bytes 45088 | tf_op jit(solution)/shard_map/ppermute | solution.py:499
  12.8 0.2 shard_map.123
  13.0 1.6 %collective-permute-start.3 = (f32[8,128]{1,0:T(8,128)S(1)}, f32[8,128]{1,0:T(8,128)S(1)}, u32[]{:S(2)}, u32[]{:S(2)}) collective-permute-start(f32[8,128]{1,0:T(8,128)S(1)} %get-tuple-element.26.refs_0_), channel_id=1, source_target_pairs={{0,2},{2,0},{1,3},{3,1},{4,6},{6,4},{5,7},{7,5},{8,10},{10,8},{9,1... | collective-permute-start | bytes 12296 | tf_op jit(solution)/shard_map/ppermute | solution.py:499
  14.5 0.0 copy-start
  14.5 1.0 %shard_map.124.refs_2_ = f32[20,8,256]{2,1,0:T(8,128)S(1)} custom-call(f32[20,8,256]{2,1,0:T(8,128)S(1)} %get-tuple-element.27.weights_ref, f32[8,256]{1,0:T(8,128)S(1)} %copy-done.3, f32[8,8,256]{2,1,0:T(8,128)S(1)} %get-tuple-element.28.forward_ref, f32[8,8,256]{2,1,0:T(8,128)S(1)} %get-tuple-element.29.reverse_ref), custom_call_target="tpu_custom_call" | custom-call | flops 100000 | bytes 100000 | tf_op jit(solution)/shard_map/pallas_call | solution.py:572
  15.6 1.1 %collective-permute-done.3.refs_1_ = f32[8,128]{1,0:T(8,128)S(1)} collective-permute-done((f32[8,128]{1,0:T(8,128)S(1)}, f32[8,128]{1,0:T(8,128)S(1)}, u32[]{:S(2)}, u32[]{:S(2)}) %collective-permute-start.3) | collective-permute-done | bytes 4128 | tf_op jit(solution)/shard_map/ppermute | solution.py:499
  16.6 0.0 copy-done
  16.6 0.3 shard_map.125.refs_0_
  16.9 0.1 collective-permute-start.4
  17.0 1.2 %collective-permute-done.4.refs_1_ = f32[16,256]{1,0:T(8,128)S(1)} collective-permute-done((f32[16,256]{1,0:T(8,128)S(1)}, f32[16,256]{1,0:T(8,128)S(1)}, u32[]{:S(2)}, u32[]{:S(2)}) %collective-permute-start.4) | collective-permute-done | bytes 16416 | tf_op jit(solution)/shard_map/ppermute | solution.py:505
  18.2 0.9 %shard_map.126 = (f32[16,256]{1,0:T(8,128)}, f32[20,8,256]{2,1,0:T(8,128)S(1)}, f32[8,128]{1,0:T(8,128)S(1)}) custom-call(f32[16,256]{1,0:T(8,128)S(1)} %shard_map.125.refs_0_, f32[16,256]{1,0:T(8,128)S(1)} %collective-permute-done.4.refs_1_, bf16[2,20,8,256]{3,2,1,0:T(8,128)(2,1)S(1)} %copy-done, bf16[256,512]{1,0:T(8,128)(2,1)S(1)} %get-tuple-element.30.refs_3_, ...), custom_call_target="tpu_custom_call" | custom-call | flops 100000 | bytes 100000 | tf_op jit(solution)/shard_map/pallas_call | solution.py:577
  19.1 1.5 %collective-permute-start.5 = (f32[8,128]{1,0:T(8,128)S(1)}, f32[8,128]{1,0:T(8,128)S(1)}, u32[]{:S(2)}, u32[]{:S(2)}) collective-permute-start(f32[8,128]{1,0:T(8,128)S(1)} %get-tuple-element.33.refs_0_), channel_id=1, source_target_pairs={{0,2},{2,0},{1,3},{3,1},{4,6},{6,4},{5,7},{7,5},{8,10},{10,8},{9,1... | collective-permute-start | bytes 12296 | tf_op jit(solution)/shard_map/ppermute | solution.py:499
  20.6 0.0 copy-start.1
  20.6 0.0 copy-start.5
  20.6 1.0 %shard_map.127.refs_2_ = f32[20,8,256]{2,1,0:T(8,128)S(1)} custom-call(f32[20,8,256]{2,1,0:T(8,128)S(1)} %get-tuple-element.34.weights_ref, f32[8,256]{1,0:T(8,128)S(1)} %copy-done.3, f32[8,8,256]{2,1,0:T(8,128)S(1)} %get-tuple-element.28.forward_ref, f32[8,8,256]{2,1,0:T(8,128)S(1)} %get-tuple-element.29.reverse_ref), custom_call_target="tpu_custom_call" | custom-call | flops 100000 | bytes 100000 | tf_op jit(solution)/shard_map/pallas_call | solution.py:582
  21.6 1.1 %collective-permute-done.5.refs_1_ = f32[8,128]{1,0:T(8,128)S(1)} collective-permute-done((f32[8,128]{1,0:T(8,128)S(1)}, f32[8,128]{1,0:T(8,128)S(1)}, u32[]{:S(2)}, u32[]{:S(2)}) %collective-permute-start.5) | collective-permute-done | bytes 4128 | tf_op jit(solution)/shard_map/ppermute | solution.py:499
  22.7 0.0 copy-done.1
  22.7 0.0 copy-done.5
  22.7 0.4 %shard_map.128 = (f32[20,8,256]{2,1,0:T(8,128)S(1)}, f32[168,128]{1,0:T(8,128)S(1)}) custom-call(f32[8,128]{1,0:T(8,128)S(1)} %get-tuple-element.33.refs_0_, f32[8,128]{1,0:T(8,128)S(1)} %collective-permute-done.5.refs_1_, f32[20,8,256]{2,1,0:T(8,128)S(1)} %shard_map.127.refs_2_, f32[5,8,256]{2,1,0:T(8,128)S(1)} %get-tuple-element.25.refs_6_.refs_3_.refs_7_, ...), custom_call_target="tpu_custom_call" | custom-call | flops 100000 | bytes 100000 | tf_op jit(solution)/shard_map/pallas_call | solution.py:583
  23.1 1.0 %collective-permute-start.8 = (f32[168,128]{1,0:T(8,128)S(1)}, f32[168,128]{1,0:T(8,128)S(1)}, u32[]{:S(2)}, u32[]{:S(2)}) collective-permute-start(f32[168,128]{1,0:T(8,128)S(1)} %get-tuple-element.36.refs_0_), channel_id=1, source_target_pairs={{0,12},{4,0},{8,4},{12,8},{1,13},{5,1},{9,5},{13,9},{2,14},{6,2},{... | collective-permute-start | bytes 258056 | tf_op jit(solution)/shard_map/ppermute | solution.py:499
  24.1 0.3 collective-permute-start.7
  24.4 1.9 %collective-permute-start.6 = (f32[168,128]{1,0:T(8,128)S(1)}, f32[168,128]{1,0:T(8,128)S(1)}, u32[]{:S(2)}, u32[]{:S(2)}) collective-permute-start(f32[168,128]{1,0:T(8,128)S(1)} %get-tuple-element.36.refs_0_), channel_id=1, source_target_pairs={{0,4},{4,8},{8,12},{12,0},{1,5},{5,9},{9,13},{13,1},{2,6},{6,10},{... | collective-permute-start | bytes 258056 | tf_op jit(solution)/shard_map/ppermute | solution.py:499
  26.3 1.5 %collective-permute-done.8.refs_3_ = f32[168,128]{1,0:T(8,128)S(1)} collective-permute-done((f32[168,128]{1,0:T(8,128)S(1)}, f32[168,128]{1,0:T(8,128)S(1)}, u32[]{:S(2)}, u32[]{:S(2)}) %collective-permute-start.8) | collective-permute-done | bytes 86048 | tf_op jit(solution)/shard_map/ppermute | solution.py:499
  27.9 4.4 %collective-permute-done.7.refs_2_ = f32[168,128]{1,0:T(8,128)S(1)} collective-permute-done((f32[168,128]{1,0:T(8,128)S(1)}, f32[168,128]{1,0:T(8,128)S(1)}, u32[]{:S(2)}, u32[]{:S(2)}) %collective-permute-start.7) | collective-permute-done | bytes 86048 | tf_op jit(solution)/shard_map/ppermute | solution.py:499
  32.3 0.0 collective-permute-done.6.refs_1_
  32.3 0.0 copy-start.4
  32.3 0.2 shard_map.129
  32.5 0.1 collective-permute-start.9
  32.5 1.2 %collective-permute-done.9 = f32[8,128]{1,0:T(8,128)S(1)} collective-permute-done((f32[8,128]{1,0:T(8,128)S(1)}, f32[8,128]{1,0:T(8,128)S(1)}, u32[]{:S(2)}, u32[]{:S(2)}) %collective-permute-start.9) | collective-permute-done | bytes 4128 | tf_op jit(solution)/shard_map/ppermute | solution.py:505
  33.7 1.3 %collective-permute-start.10 = (f32[8,128]{1,0:T(8,128)S(1)}, f32[8,128]{1,0:T(8,128)S(1)}, u32[]{:S(2)}, u32[]{:S(2)}) collective-permute-start(f32[8,128]{1,0:T(8,128)S(1)} %add.3.refs_0_), channel_id=1, source_target_pairs={{0,3},{1,2},{2,1},{3,0},{4,7},{5,6},{6,5},{7,4},{8,11},{9,10},{10,... | collective-permute-start | bytes 12296 | tf_op jit(solution)/shard_map/ppermute | solution.py:511
  35.0 1.8 %collective-permute-done.10.refs_1_ = f32[8,128]{1,0:T(8,128)S(1)} collective-permute-done((f32[8,128]{1,0:T(8,128)S(1)}, f32[8,128]{1,0:T(8,128)S(1)}, u32[]{:S(2)}, u32[]{:S(2)}) %collective-permute-start.10) | collective-permute-done | bytes 4128 | tf_op jit(solution)/shard_map/ppermute | solution.py:511
  36.7 0.0 copy-done.4
  36.7 0.9 %shard_map.130 = (f32[20,8,256]{2,1,0:T(8,128)}, f32[20,8,256]{2,1,0:T(8,128)}) custom-call(f32[8,128]{1,0:T(8,128)S(1)} %add.3.refs_0_, f32[8,128]{1,0:T(8,128)S(1)} %collective-permute-done.10.refs_1_, f32[20,8,256]{2,1,0:T(8,128)S(1)} %get-tuple-element.39.refs_2_, f32[20,8,256]{2,1,0:T(8,128)S(1)} %copy-done.4), custom_call_target="tpu_custom_call" | custom-call | flops 100000 | bytes 100000 | tf_op jit(solution)/shard_map/pallas_call | solution.py:593
  (1 shorter events, 0.0 us)
Async XLA Ops:
  0.6 7.3 %copy-start.2 = (f32[20,8,256]{2,1,0:T(8,128)S(1)}, f32[20,8,256]{2,1,0:T(8,128)}, u32[]{:S(2)}) copy-start(f32[20,8,256]{2,1,0:T(8,128)} %refs_8_.1) | copy-start | bytes 491524
  0.6 7.3 %copy-start.6 = (s32[1,1,512]{2,1,0:T(1,128)S(1)}, s32[1,1,512]{2,1,0:T(1,128)}, u32[]{:S(2)}) copy-start(s32[1,1,512]{2,1,0:T(1,128)} %param.14) | copy-start | bytes 6148
  0.7 7.3 %copy-start.7 = (s32[1,1,512]{2,1,0:T(1,128)S(1)}, s32[1,1,512]{2,1,0:T(1,128)}, u32[]{:S(2)}) copy-start(s32[1,1,512]{2,1,0:T(1,128)} %param.15) | copy-start | bytes 6148
  0.7 7.3 %copy-start.8 = (f32[1,1,512]{2,1,0:T(1,128)S(1)}, f32[1,1,512]{2,1,0:T(1,128)}, u32[]{:S(2)}) copy-start(f32[1,1,512]{2,1,0:T(1,128)} %param.16) | copy-start | bytes 6148
  0.7 7.3 %copy-start.9 = (f32[1,1,512]{2,1,0:T(1,128)S(1)}, f32[1,1,512]{2,1,0:T(1,128)}, u32[]{:S(2)}) copy-start(f32[1,1,512]{2,1,0:T(1,128)} %param.17) | copy-start | bytes 6148
  1.8 6.2 %copy-start.3 = (f32[8,256]{1,0:T(8,128)S(1)}, f32[8,256]{1,0:T(8,128)}, u32[]{:S(2)}) copy-start(f32[8,256]{1,0:T(8,128)} %refs_4_.3) | copy-start | bytes 24580
  1.8 7.4 %collective-permute-start.2 = (f32[88,128]{1,0:T(8,128)S(1)}, f32[88,128]{1,0:T(8,128)S(1)}, u32[]{:S(2)}, u32[]{:S(2)}) collective-permute-start(f32[88,128]{1,0:T(8,128)S(1)} %get-tuple-element.23.refs_0_.refs_4_), channel_id=1, source_target_pairs={{0,12},{4,0},{8,4},{12,8},{1,13},{5,1},{9,5},{13,9},{2,14},{6,2},{... | collective-permute-start | bytes 135176 | tf_op jit(solution)/shard_map/ppermute | solution.py:499
  6.9 4.9 %collective-permute-start.1 = (f32[88,128]{1,0:T(8,128)S(1)}, f32[88,128]{1,0:T(8,128)S(1)}, u32[]{:S(2)}, u32[]{:S(2)}) collective-permute-start(f32[88,128]{1,0:T(8,128)S(1)} %get-tuple-element.23.refs_0_.refs_4_), channel_id=1, source_target_pairs={{0,8},{4,12},{8,0},{12,4},{1,9},{5,13},{9,1},{13,5},{2,10},{6,14},... | collective-permute-start | bytes 135176 | tf_op jit(solution)/shard_map/ppermute | solution.py:499
  6.9 5.8 %collective-permute-start = (f32[88,128]{1,0:T(8,128)S(1)}, f32[88,128]{1,0:T(8,128)S(1)}, u32[]{:S(2)}, u32[]{:S(2)}) collective-permute-start(f32[88,128]{1,0:T(8,128)S(1)} %get-tuple-element.23.refs_0_.refs_4_), channel_id=1, source_target_pairs={{0,4},{4,8},{8,12},{12,0},{1,5},{5,9},{9,13},{13,1},{2,6},{6,10},{... | collective-permute-start | bytes 135176 | tf_op jit(solution)/shard_map/ppermute | solution.py:499
  13.0 3.7 %collective-permute-start.3 = (f32[8,128]{1,0:T(8,128)S(1)}, f32[8,128]{1,0:T(8,128)S(1)}, u32[]{:S(2)}, u32[]{:S(2)}) collective-permute-start(f32[8,128]{1,0:T(8,128)S(1)} %get-tuple-element.26.refs_0_), channel_id=1, source_target_pairs={{0,2},{2,0},{1,3},{3,1},{4,6},{6,4},{5,7},{7,5},{8,10},{10,8},{9,1... | collective-permute-start | bytes 12296 | tf_op jit(solution)/shard_map/ppermute | solution.py:499
  14.5 2.1 %copy-start = (bf16[2,20,8,256]{3,2,1,0:T(8,128)(2,1)S(1)}, bf16[2,20,8,256]{3,2,1,0:T(8,128)(2,1)}, u32[]{:S(2)}) copy-start(bf16[2,20,8,256]{3,2,1,0:T(8,128)(2,1)} %refs_2_.1) | copy-start | bytes 491524
  16.9 1.2 %collective-permute-start.4 = (f32[16,256]{1,0:T(8,128)S(1)}, f32[16,256]{1,0:T(8,128)S(1)}, u32[]{:S(2)}, u32[]{:S(2)}) collective-permute-start(f32[16,256]{1,0:T(8,128)S(1)} %shard_map.125.refs_0_), channel_id=1, source_target_pairs={{0,1},{1,0},{2,3},{3,2},{4,5},{5,4},{6,7},{7,6},{8,9},{9,8},{10,11... | collective-permute-start | bytes 49160 | tf_op jit(solution)/shard_map/ppermute | solution.py:505
  19.1 3.6 %collective-permute-start.5 = (f32[8,128]{1,0:T(8,128)S(1)}, f32[8,128]{1,0:T(8,128)S(1)}, u32[]{:S(2)}, u32[]{:S(2)}) collective-permute-start(f32[8,128]{1,0:T(8,128)S(1)} %get-tuple-element.33.refs_0_), channel_id=1, source_target_pairs={{0,2},{2,0},{1,3},{3,1},{4,6},{6,4},{5,7},{7,5},{8,10},{10,8},{9,1... | collective-permute-start | bytes 12296 | tf_op jit(solution)/shard_map/ppermute | solution.py:499
  20.6 2.1 %copy-start.1 = (f32[20,8,256]{2,1,0:T(8,128)S(1)}, f32[20,8,256]{2,1,0:T(8,128)}, u32[]{:S(2)}) copy-start(f32[20,8,256]{2,1,0:T(8,128)} %refs_7_.1) | copy-start | bytes 491524
  20.6 2.1 %copy-start.5 = (f32[8,256]{1,0:T(8,128)S(1)}, f32[8,256]{1,0:T(8,128)}, u32[]{:S(2)}) copy-start(f32[8,256]{1,0:T(8,128)} %refs_9_.1) | copy-start | bytes 24580
  23.1 4.7 %collective-permute-start.8 = (f32[168,128]{1,0:T(8,128)S(1)}, f32[168,128]{1,0:T(8,128)S(1)}, u32[]{:S(2)}, u32[]{:S(2)}) collective-permute-start(f32[168,128]{1,0:T(8,128)S(1)} %get-tuple-element.36.refs_0_), channel_id=1, source_target_pairs={{0,12},{4,0},{8,4},{12,8},{1,13},{5,1},{9,5},{13,9},{2,14},{6,2},{... | collective-permute-start | bytes 258056 | tf_op jit(solution)/shard_map/ppermute | solution.py:499
  24.1 8.2 %collective-permute-start.7 = (f32[168,128]{1,0:T(8,128)S(1)}, f32[168,128]{1,0:T(8,128)S(1)}, u32[]{:S(2)}, u32[]{:S(2)}) collective-permute-start(f32[168,128]{1,0:T(8,128)S(1)} %get-tuple-element.36.refs_0_), channel_id=1, source_target_pairs={{0,8},{4,12},{8,0},{12,4},{1,9},{5,13},{9,1},{13,5},{2,10},{6,14},... | collective-permute-start | bytes 258056 | tf_op jit(solution)/shard_map/ppermute | solution.py:499
  24.4 7.9 %collective-permute-start.6 = (f32[168,128]{1,0:T(8,128)S(1)}, f32[168,128]{1,0:T(8,128)S(1)}, u32[]{:S(2)}, u32[]{:S(2)}) collective-permute-start(f32[168,128]{1,0:T(8,128)S(1)} %get-tuple-element.36.refs_0_), channel_id=1, source_target_pairs={{0,4},{4,8},{8,12},{12,0},{1,5},{5,9},{9,13},{13,1},{2,6},{6,10},{... | collective-permute-start | bytes 258056 | tf_op jit(solution)/shard_map/ppermute | solution.py:499
  32.3 4.4 %copy-start.4 = (f32[20,8,256]{2,1,0:T(8,128)S(1)}, f32[20,8,256]{2,1,0:T(8,128)}, u32[]{:S(2)}) copy-start(f32[20,8,256]{2,1,0:T(8,128)} %refs_3_.1) | copy-start | bytes 491524
  32.5 1.2 %collective-permute-start.9 = (f32[8,128]{1,0:T(8,128)S(1)}, f32[8,128]{1,0:T(8,128)S(1)}, u32[]{:S(2)}, u32[]{:S(2)}) collective-permute-start(f32[8,128]{1,0:T(8,128)S(1)} %get-tuple-element.38), channel_id=1, source_target_pairs={{0,1},{1,0},{2,3},{3,2},{4,5},{5,4},{6,7},{7,6},{8,9},{9,8},{10,11... | collective-permute-start | bytes 12296 | tf_op jit(solution)/shard_map/ppermute | solution.py:505
  33.7 3.0 %collective-permute-start.10 = (f32[8,128]{1,0:T(8,128)S(1)}, f32[8,128]{1,0:T(8,128)S(1)}, u32[]{:S(2)}, u32[]{:S(2)}) collective-permute-start(f32[8,128]{1,0:T(8,128)S(1)} %add.3.refs_0_), channel_id=1, source_target_pairs={{0,3},{1,2},{2,1},{3,0},{4,7},{5,6},{6,5},{7,4},{8,11},{9,10},{10,... | collective-permute-start | bytes 12296 | tf_op jit(solution)/shard_map/ppermute | solution.py:511
